TPU v7x, 256 devices: a whole 4x4x8 slice. The times are simulated.
256 devices in a mesh: dp: 32 (over y, z_lo, core), cent: 8 (over x, z_hi).
Axes of the slice: x: 4, y: 4, z: 8 (z_hi: 2, z_lo: 4; z = z_hi * 4 + z_lo), core: 2. Of those that a mesh axis runs over, the one named last changes fastest.
Arguments:
- hidden: bfloat16 [5632, 11008], P('dp', 'cent'), may hold values from -6 to 6
- residual: bfloat16 [5632, 4096], P('dp', 'cent'), may hold values from -6 to 6
- down_weight: bfloat16 [11008, 4096], P('cent', 'dp'), may hold values from -0.0546875 to 0.0546875
- gain: float32 [4096], P('cent'), may hold values from 0.1 to 1.9
- proj_weight: bfloat16 [4096, 1024], P('cent'), may hold values from -0.09375 to 0.09375
- centroids: bfloat16 [131072, 1024], P(('dp', 'cent')), may hold values from -24 to 24
Outputs:
- weighted: float32 [131072, 1024], P(('dp', 'cent'))
- counts: float32 [131072], P(('dp', 'cent'))
All inputs are finite; a program needn't handle non-finite values.
Results may differ from a plain program's by a relative error of at most 0.011.
Values may be sent and summed in bfloat16 or wider, within the bound.
A program may use at most 128 MiB of HBM per device.

v0:
```python
import math

import jax
import jax.numpy as jnp
from jax import lax
from jax.sharding import PartitionSpec as P


def body(hidden, residual, down_weight, gain, proj_weight, centroids):
    partial_layer = jnp.dot(
        hidden,
        lax.all_gather(down_weight, "dp", axis=1, tiled=True),
        preferred_element_type=jnp.float32,
    )
    layer_out = lax.psum_scatter(partial_layer, "cent", scatter_dimension=1, tiled=True)
    normed = ((layer_out + residual.astype(jnp.float32)) * gain).astype(jnp.bfloat16)
    partial_embed = jnp.dot(normed, proj_weight, preferred_element_type=jnp.float32)
    embed_width = proj_weight.shape[1]
    embed_full = lax.psum(partial_embed, "cent")
    scaled = (
        embed_full * lax.rsqrt(jnp.mean(embed_full * embed_full, axis=1, keepdims=True) + 1e-06)
    ).astype(jnp.bfloat16)
    gathered = lax.all_gather(scaled, "dp", axis=0, tiled=True)
    inverse = 1.0 / (math.sqrt(embed_width) * 0.05)
    scores = (
        lax.dot_general(
            gathered, centroids, (((1,), (1,)), ((), ())), preferred_element_type=jnp.float32
        )
        * inverse
    )
    local_max = jnp.max(scores, axis=1)
    row_max = lax.pmax(local_max, ("dp", "cent"))
    row_total = lax.psum(jnp.sum(jnp.exp(scores - row_max[:, None]), axis=1), ("dp", "cent"))
    log_total = row_max + jnp.log(row_total)
    probability = jnp.exp(scores - log_total[:, None])
    scale_up = centroids.shape[0] * lax.axis_size("dp") * lax.axis_size("cent") / gathered.shape[0]
    counts = scale_up * jnp.sum(probability, axis=0)
    prob_low = probability.astype(jnp.bfloat16)
    weighted = scale_up * lax.dot_general(
        prob_low, gathered, (((0,), (0,)), ((), ())), preferred_element_type=jnp.float32
    )
    return (weighted, counts)


def solution(mesh):
    in_specs = (
        P("dp", "cent"),
        P("dp", "cent"),
        P("cent", "dp"),
        P("cent"),
        P("cent", None),
        P(("dp", "cent"), None),
    )
    out_specs = (P(("dp", "cent"), None), P(("dp", "cent")))
    return jax.shard_map(body, mesh=mesh, in_specs=in_specs, out_specs=out_specs, check_vma=False)
```

profile of v0, /device:TPU:1, one launch (start us, length us, event | category | flops | bytes accessed | tf_op | source)
XLA Modules:
  0.0 617.1 jit_solution(13492038344672853306)
XLA Ops:
  7.2 0.0 copy-start
  7.2 0.0 copy-start.1
  7.2 0.0 copy-start.3
  7.2 0.0 copy-start.2
  7.2 0.0 all-gather.3.cloned.1.call-start
  7.3 0.7 all-gather.3.cloned.1.call-update
  7.9 0.0 reduce-scatter.2.cloned.1.call-start
  8.0 105.2 %all-gather.3.cloned.1.call-done = bf16[1376,4096]{1,0:T(8,128)(2,1)} async-done(((bf16[1376,128]{1,0:T(8,128)(2,1)}), bf16[1376,4096]{1,0:T(8,128)(2,1)}) %all-gather.3.cloned.1.call-update) | async-done | bytes 11272208 | tf_op jit(solution)/shard_map/all_gather | solution.py:12
  113.2 8.5 %fusion.11 = f32[176,4096]{1,0:T(8,128)} fusion(bf16[176,1376]{1,0:T(8,128)(2,1)} %param.6, bf16[1376,4096]{1,0:T(8,128)(2,1)} %all-gather.3.cloned.1.call-done), kind=kOutput, calls=%fused_computation.17 | convolution fusion | flops 1983905792 | bytes 14640128 | tf_op jit(solution)/shard_map/dot_general | solution.py:10
  121.7 0.0 reduce-scatter.2.cloned.1.call-update
  121.7 0.0 all-reduce.2.cloned.1.call-start
  121.8 103.8 %reduce-scatter.2.cloned.1.call-done = f32[176,512]{1,0:T(8,128)} async-done(((f32[176,4096]{1,0:T(8,128)}), f32[176,512]{1,0:T(8,128)}) %reduce-scatter.2.cloned.1.call-update) | async-done | bytes 360464 | tf_op jit(solution)/shard_map/reduce_scatter | solution.py:15
  225.6 0.0 copy-done.1
  225.6 0.0 copy-done.3
  225.6 0.0 copy-done.2
  225.6 2.2 fusion.8
  227.8 0.0 all-reduce.2.cloned.1.call-update
  227.8 0.0 all-gather.5.cloned.1.call-start
  227.8 112.2 %all-reduce.2.cloned.1.call-done = f32[176,1024]{1,0:T(8,128)} async-done(((f32[176,1024]{1,0:T(8,128)}), f32[176,1024]{1,0:T(8,128)}) %all-reduce.2.cloned.1.call-update) | async-done | bytes 720912 | tf_op jit(solution)/shard_map/psum | solution.py:19
  340.1 1.2 multiply_reduce_fusion
  341.3 2.0 multiply_convert_fusion
  343.3 0.0 all-gather.5.cloned.1.call-update
  343.3 78.9 %all-gather.5.cloned.1.call-done = bf16[5632,1024]{1,0:T(8,128)(2,1)} async-done(((bf16[176,1024]{1,0:T(8,128)(2,1)}), bf16[5632,1024]{1,0:T(8,128)(2,1)}) %all-gather.5.cloned.1.call-update) | async-done | bytes 11534352 | tf_op jit(solution)/shard_map/all_gather | solution.py:23
  422.2 0.0 copy-done
  422.2 13.2 %fusion.10 = (f32[5632]{0:T(1024)S(1)}, f32[5632,512]{0,1:T(8,128)}) fusion(bf16[5632,1024]{1,0:T(8,128)(2,1)} %all-gather.5.cloned.1.call-done, bf16[512,1024]{1,0:T(8,128)(2,1)S(1)} %copy-done), kind=kOutput, calls=%fused_computation.16 | convolution fusion | flops 5911341568 | bytes 24139776 | tf_op jit(solution)/shard_map/dot_general | solution.py:26
  435.3 76.1 %pmax.7 = f32[5632]{0:T(1024)S(1)} all-reduce(f32[5632]{0:T(1024)S(1)} %get-tuple-element.2), channel_id=1, replica_groups=mesh['dp'=32,'cent'=8] {'dp','cent'}, use_global_device_ids=true, to_apply=%region_4.0 | all-reduce | flops 5632 | bytes 45056 | tf_op jit(solution)/shard_map/pmax | solution.py:32
  511.4 6.0 exponential_reduce_fusion
  517.4 73.3 %psum.15 = f32[5632]{0:T(1024)S(1)} all-reduce(f32[5632]{0:T(1024)S(1)} %exponential_reduce_fusion), channel_id=1, replica_groups=mesh['dp'=32,'cent'=8] {'dp','cent'}, use_global_device_ids=true, to_apply=%region_6.0 | all-reduce | flops 5632 | bytes 45056 | tf_op jit(solution)/shard_map/psum | solution.py:33
  590.7 6.0 fusion
  596.7 0.6 broadcast_multiply_fusion
  597.3 13.3 %fusion.5 = f32[512,1024]{1,0:T(8,128)} fusion(bf16[5632,1024]{1,0:T(8,128)(2,1)} %all-gather.5.cloned.1.call-done, f32[5632,512]{0,1:T(8,128)} %get-tuple-element.3, f32[5632]{0:T(1024)S(1)} %log_add_fusion), kind=kOutput, calls=%fused_computation.7 | convolution fusion | flops 5911871488 | bytes 25188352 | tf_op jit(solution)/shard_map/dot_general | solution.py:39
  (2 shorter events, 0.0 us)
Async XLA Ops:
  7.2 415.0 %copy-start = (bf16[512,1024]{1,0:T(8,128)(2,1)S(1)}, bf16[512,1024]{1,0:T(8,128)(2,1)}, u32[]{:S(2)}) copy-start(bf16[512,1024]{1,0:T(8,128)(2,1)} %param.11) | copy-start | bytes 3145732
  7.2 218.4 %copy-start.1 = (bf16[512,1024]{1,0:T(8,128)(2,1)S(1)}, bf16[512,1024]{1,0:T(8,128)(2,1)}, u32[]{:S(2)}) copy-start(bf16[512,1024]{1,0:T(8,128)(2,1)} %param.10) | copy-start | bytes 3145732
  7.2 218.4 %copy-start.3 = (f32[512]{0:T(512)S(1)}, f32[512]{0:T(512)}, u32[]{:S(2)}) copy-start(f32[512]{0:T(512)} %param.9) | copy-start | bytes 6148
  7.2 218.4 %copy-start.2 = (bf16[176,512]{1,0:T(8,128)(2,1)S(1)}, bf16[176,512]{1,0:T(8,128)(2,1)}, u32[]{:S(2)}) copy-start(bf16[176,512]{1,0:T(8,128)(2,1)} %param.7) | copy-start | bytes 540676
  7.2 106.0 %all-gather.3.cloned.1.call-start = ((), (), s32[]{:S(2)}) async-start(), calls=%async_computation.1 | async-start | bytes 11624448 | tf_op jit(solution)/shard_map/all_gather | solution.py:12
  7.9 217.6 %reduce-scatter.2.cloned.1.call-start = ((), (), s32[]{:S(2)}) async-start(), calls=%async_computation.2 | async-start | bytes 3244032 | tf_op jit(solution)/shard_map/reduce_scatter | solution.py:15
  121.7 218.3 %all-reduce.2.cloned.1.call-start = ((), (), s32[]{:S(2)}) async-start(), calls=%async_computation.3 | async-start | bytes 1441792 | tf_op jit(solution)/shard_map/psum | solution.py:19
  227.8 194.4 %all-gather.5.cloned.1.call-start = ((), (), s32[]{:S(2)}) async-start(), calls=%async_computation.4 | async-start | bytes 11894784 | tf_op jit(solution)/shard_map/all_gather | solution.py:23
Sparse Core Ops, SparseCore 0:
  9.8 103.3 all-gather.2
  121.8 103.6 reduce-scatter.1
  228.8 111.2 all-reduce.1
  343.4 78.7 all-gather.4
where the time goes:
time: 618 us; the launch traced here: 617 us
  waiting for transfers between devices  401 us (65%)
  blocking collectives  149 us (24%)
  matrix products  37.1 us (6%)
  other arithmetic  15.8 us (3%)
  between operations  13.8 us (2%)
    psum x1, waiting for transfers between devices, body(): embed_full = lax.psum(partial_embed, 'cent')  112 us
    all_gather x1, waiting for transfers between devices, body(): lax.all_gather(down_weight, 'dp', axis=1, tiled=True)  105 us
    reduce_scatter x1, waiting for transfers between devices, body(): lax.psum_scatter(partial_layer, 'cent', scatter_dimension=1, tiled=True)  104 us
    all_gather x1, waiting for transfers between devices, body(): gathered = lax.all_gather(scaled, 'dp', axis=0, tiled=True)  78.9 us
    pmax x1, blocking collectives, body(): row_max = lax.pmax(local_max, ('dp', 'cent'))  76.1 us
    psum x1, blocking collectives, body(): lax.psum(jnp.sum(jnp.exp(scores - row_max[:, None]), axis=1), ('dp', 'cen...  73.3 us
    dot_general x1, matrix products, body(): lax.dot_general(prob_low, gathered, (((0,), (0,)), ((), ())), preferred_e...  13.3 us
    dot_general x1, matrix products, body(): lax.dot_general(gathered, centroids, (((1,), (1,)), ((), ())), preferred_...  13.2 us
  transfers between devices with their start and end apart: 4, of which 4 were waited for; matrix products, arithmetic and copies ran while one was open for 0% of the time, Pallas kernels for 0%

commit v1 on v0

v1 whole, which is shorter than its diff:
```python
import functools
import math

import jax
import jax.numpy as jnp
from jax import lax
from jax.experimental import pallas as pl
from jax.experimental.pallas import tpu as pltpu
from jax.sharding import PartitionSpec as P

MESH = pl.DeviceIdType.MESH
NX, NY, NZ = 4, 4, 8
NL = 4
LANES = 128


def coordinates():
    dp, cent = lax.axis_index("dp"), lax.axis_index("cent")
    y, low, core = dp // (2 * NL), (dp // 2) % NL, dp % 2
    return cent // 2, y, (cent % 2) * NL + low, core


def device(x, y, z, core):
    return (y * (2 * NL) + (z % NL) * 2 + core, x * 2 + z // NL)


def aligned(value, multiple):
    return pl.multiple_of(value, multiple)


def greet(peers):
    barrier = pltpu.get_barrier_semaphore()
    for peer in peers:
        pl.semaphore_signal(barrier, inc=1, device_id=peer, device_id_type=MESH)
    pl.semaphore_wait(barrier, len(peers))


def gather_plan(rows, x, y, z):
    low, high = z % NL, z // NL
    r0, r1, r2 = rows
    b0, b1, b2 = 0, 16 * r0, 16 * (r0 + r1)

    def box(row, count, col, width):
        return (aligned(row, 16), count, aligned(col, LANES), width)

    def column(zc, xc):
        return ((zc // NL) * NX + xc) * LANES

    first = (
        ("x", lambda i: [box(b0 + (low * NY + y) * r0, r0, (high * NX + i) * LANES, LANES)]),
        ("y", lambda i: [box(b0 + (low * NY + i) * r0, r0, high * NX * LANES, NX * LANES)]),
        ("z", lambda i: [box(b0 + (i % NL) * NY * r0, NY * r0, (i // NL) * NX * LANES, NX * LANES)]),
    )
    second = (
        ("y", lambda i: [box(b1 + (low * NY + i) * r1, r1, column(z, x), LANES)]),
        ("z", lambda i: [box(b1 + (i % NL) * NY * r1, NY * r1, column(i, x), LANES)]),
        ("x", lambda i: [box(b1, 16 * r1, (h * NX + i) * LANES, LANES) for h in range(2)]),
    )
    third = (
        ("z", lambda i: [box(b2 + (y * NL + i % NL) * r2, r2, column(i, x), LANES)]),
        ("x", lambda i: [box(b2 + y * NL * r2, NL * r2, (h * NX + i) * LANES, LANES) for h in range(2)]),
        ("y", lambda i: [box(b2 + i * NL * r2, NL * r2, 0, 2 * NX * LANES)]),
    )
    own = (
        (0, r0, aligned(b0 + (low * NY + y) * r0, 16)),
        (r0, r1, aligned(b1 + (low * NY + y) * r1, 16)),
        (r0 + r1, r2, aligned(b2 + (y * NL + low) * r2, 16)),
    )
    return (first, second, third), own, aligned(column(z, x), LANES)


def half(box, which):
    row, count, col, width = box
    upper = (count // 2 + 15) // 16 * 16
    return (row, upper, col, width) if which == 0 else (aligned(row + upper, 16), count - upper, col, width)


def ring_steps(stages, position, size):
    steps = []
    for axis, boxes in stages:
        n, me = size[axis], position[axis]
        for s in range(1, n // 2 + 1):
            sends = []
            for which, way in ((0, 1), (1, -1)):
                sent = boxes((me - way * (s - 1) + n) % n)
                got = boxes((me - way * s + n) % n)
                if s == n // 2:
                    sent, got = [half(b, which) for b in sent], [half(b, which) for b in got]
                sends.append((way, axis, sent, got))
            steps.append(sends)
    return steps


def main_kernel(
    rows, chunk, inverse, scale_up,
    block_ref, cent_ref, weighted_ref, counts_ref,
    embed, cents, expo, prob, maxima, logs, total, heard, other_sum, own_sum, other_count, sent_count,
    send_sem, recv_sem, local_sem, cent_sem, lse_send, lse_recv, out_sem,
):
    x, y, z, core = coordinates()
    here = {"x": x, "y": y, "z": z}
    size = {"x": NX, "y": NY, "z": NZ}

    def at(axis, value):
        place = dict(here)
        place[axis] = value
        return device(place["x"], place["y"], place["z"], core)

    mate = device(x, y, z, 1 - core)
    peers = [mate]
    for axis in "xyz":
        peers += [at(axis, (here[axis] + i) % size[axis]) for i in range(1, size[axis])]
    greet(peers)

    colours, own, own_col = gather_plan(rows, x, y, z)
    local = []
    for i, (start, count, row) in enumerate(own):
        local.append(pltpu.make_async_copy(
            block_ref.at[pl.ds(start, count), :],
            embed.at[pl.ds(row, count), pl.ds(own_col, LANES)],
            local_sem.at[i],
        ))
    per = cent_ref.shape[0]
    mine, theirs = aligned(core * per, 256), aligned((1 - core) * per, 256)
    for c in range(8):
        local.append(pltpu.make_async_copy(
            cent_ref.at[:, pl.ds(c * LANES, LANES)],
            cents.at[pl.ds(mine, per), pl.ds(((c % 2) * NX + c // 2) * LANES, LANES)],
            local_sem.at[3 + c],
        ))
    for copy in local:
        copy.start()
    for copy in local:
        copy.wait()

    def view(box):
        row, count, col, width = box
        return embed.at[pl.ds(row, count), pl.ds(col, width)]

    plans = [ring_steps(stages, here, size) for stages in colours]
    slot = 0
    arriving, sent = [[] for _ in plans], []
    for t in range(len(plans[0])):
        for c, plan in enumerate(plans):
            for copy in arriving[c]:
                copy.wait_recv()
            arriving[c] = []
            for way, axis, out_boxes, in_boxes in plan[t]:
                target = at(axis, (here[axis] + way + size[axis]) % size[axis])
                for o, i in zip(out_boxes, in_boxes):
                    send = pltpu.make_async_remote_copy(
                        src_ref=view(o), dst_ref=view(o), send_sem=send_sem.at[slot],
                        recv_sem=recv_sem.at[slot], device_id=target, device_id_type=MESH)
                    send.start()
                    sent.append(send)
                    arriving[c].append(pltpu.make_async_remote_copy(
                        src_ref=view(i), dst_ref=view(i), send_sem=send_sem.at[slot],
                        recv_sem=recv_sem.at[slot], device_id=target, device_id_type=MESH))
                    slot += 1
        if t == 0:
            share = pltpu.make_async_remote_copy(
                src_ref=cents.at[pl.ds(mine, per), :], dst_ref=cents.at[pl.ds(mine, per), :],
                send_sem=cent_sem.at[0], recv_sem=cent_sem.at[1], device_id=mate, device_id_type=MESH)
            share.start()
    for copies in arriving:
        for copy in copies:
            copy.wait_recv()
    for copy in sent:
        copy.wait_send()
    share.wait_send()
    pltpu.make_async_remote_copy(
        src_ref=cents.at[pl.ds(theirs, per), :], dst_ref=cents.at[pl.ds(theirs, per), :],
        send_sem=cent_sem.at[0], recv_sem=cent_sem.at[1], device_id=mate, device_id_type=MESH).wait_recv()

    count = embed.shape[0]

    def score(i, _):
        span = pl.ds(aligned(i * chunk, chunk), chunk)
        scores = lax.dot_general(
            cents[...], embed[span, :], (((1,), (1,)), ((), ())), preferred_element_type=jnp.float32
        ) * inverse
        top = jnp.max(scores, axis=0, keepdims=True)
        powers = jnp.exp(scores - top)
        expo[:, span] = powers
        maxima[:, span] = top
        logs[:, span] = top + jnp.log(jnp.sum(powers, axis=0, keepdims=True))
        return 0

    lax.fori_loop(0, count // chunk, score, 0)

    base = 0
    for stage, axis in enumerate("xyz"):
        n, me = size[axis], here[axis]
        source = logs if stage == 0 else total.at[stage - 1]
        copies = []
        for i in range(1, n):
            copies.append(pltpu.make_async_remote_copy(
                src_ref=source, dst_ref=heard.at[base + i - 1], send_sem=lse_send.at[base + i - 1],
                recv_sem=lse_recv.at[base + i - 1], device_id=at(axis, (me + i) % n), device_id_type=MESH))
        for copy in copies:
            copy.start()
        for copy in copies:
            copy.wait_recv()
        parts = [source[...]] + [heard[base + i] for i in range(n - 1)]
        top = functools.reduce(jnp.maximum, parts)
        total[stage] = top + jnp.log(sum(jnp.exp(p - top) for p in parts))
        for copy in copies:
            copy.wait_send()
        base += n - 1
    maxima[...] = jnp.exp(maxima[...] - total[2])

    width = cents.shape[0]
    lanes = 256

    def weigh(i, tally):
        span = pl.ds(aligned(i * chunk, chunk), chunk)
        p = expo[:, span] * maxima[:, span]
        prob[:, span] = p.astype(jnp.bfloat16)
        return tally + sum(p[:, j * LANES:(j + 1) * LANES] for j in range(chunk // LANES))

    tally = lax.fori_loop(0, count // chunk, weigh, jnp.zeros((width, LANES), jnp.float32))
    tally = scale_up * jnp.sum(tally.T, axis=0, keepdims=True)
    sent_count[...] = tally

    def product(start, j):
        return scale_up * lax.dot_general(
            prob[pl.ds(start, per), :], embed[:, j * lanes:(j + 1) * lanes],
            (((1,), (0,)), ((), ())), preferred_element_type=jnp.float32)

    give = []
    for j in range(embed.shape[1] // lanes):
        cols = pl.ds(j * lanes, lanes)
        own_sum[:, cols] = product(theirs, j)
        give.append(pltpu.make_async_remote_copy(
            src_ref=own_sum.at[:, cols], dst_ref=other_sum.at[:, cols], send_sem=out_sem.at[0, j],
            recv_sem=out_sem.at[1, j], device_id=mate, device_id_type=MESH))
        give[-1].start()
    give.append(pltpu.make_async_remote_copy(
        src_ref=sent_count, dst_ref=other_count, send_sem=out_sem.at[0, 4],
        recv_sem=out_sem.at[1, 4], device_id=mate, device_id_type=MESH))
    give[-1].start()
    for j in range(embed.shape[1] // lanes):
        part = product(mine, j)
        give[j].wait_recv()
        part = part + other_sum[:, j * lanes:(j + 1) * lanes]
        for b in range(lanes // LANES):
            q = j * (lanes // LANES) + b
            c = (q % NX) * 2 + q // NX
            weighted_ref[:, c * LANES:(c + 1) * LANES] = part[:, b * LANES:(b + 1) * LANES]
    give[-1].wait_recv()
    counts_ref[...] = sent_count[:, pl.ds(mine, per)] + other_count[:, pl.ds(mine, per)]
    for copy in give:
        copy.wait_send()


def cluster(block, centroids, passages):
    per, embed_width = centroids.shape
    centres = per * lax.axis_size("dp") * lax.axis_size("cent")
    part = block.shape[0]
    r2 = part // 3 // 16 * 16
    r0 = (part - r2) // 2
    rows = (r0, part - r2 - r0, r2)
    count = passages // 2
    vmem = pl.BlockSpec(memory_space=pltpu.VMEM)
    hbm = pl.BlockSpec(memory_space=pl.ANY)
    slots = 16 + 20 + 20
    weighted, counts = pl.pallas_call(
        functools.partial(main_kernel, rows, 256, 1.0 / (math.sqrt(embed_width) * 0.05), centres / passages),
        out_shape=(
            jax.ShapeDtypeStruct((per, embed_width), jnp.float32),
            jax.ShapeDtypeStruct((1, per), jnp.float32),
        ),
        in_specs=[hbm, hbm],
        out_specs=(vmem, vmem),
        scratch_shapes=[
            pltpu.VMEM((count, embed_width), jnp.bfloat16),
            pltpu.VMEM((2 * per, embed_width), jnp.bfloat16),
            pltpu.VMEM((2 * per, count), jnp.float32),
            pltpu.VMEM((2 * per, count), jnp.bfloat16),
            pltpu.VMEM((1, count), jnp.float32),
            pltpu.VMEM((1, count), jnp.float32),
            pltpu.VMEM((3, 1, count), jnp.float32),
            pltpu.VMEM((NX + NY + NZ - 3, 1, count), jnp.float32),
            pltpu.VMEM((per, embed_width), jnp.float32),
            pltpu.VMEM((per, embed_width), jnp.float32),
            pltpu.VMEM((1, 2 * per), jnp.float32),
            pltpu.VMEM((1, 2 * per), jnp.float32),
            pltpu.SemaphoreType.DMA((slots,)),
            pltpu.SemaphoreType.DMA((slots,)),
            pltpu.SemaphoreType.DMA((11,)),
            pltpu.SemaphoreType.DMA((2,)),
            pltpu.SemaphoreType.DMA((NX + NY + NZ - 3,)),
            pltpu.SemaphoreType.DMA((NX + NY + NZ - 3,)),
            pltpu.SemaphoreType.DMA((2, 5)),
        ],
        compiler_params=pltpu.CompilerParams(
            collective_id=0, has_side_effects=True, vmem_limit_bytes=60 * 1024 * 1024),
        name="cluster",
    )(block, centroids)
    return weighted, counts.reshape(per)


def body(hidden, residual, down_weight, gain, proj_weight, centroids):
    partial_layer = jnp.dot(
        hidden,
        lax.all_gather(down_weight, "dp", axis=1, tiled=True),
        preferred_element_type=jnp.float32,
    )
    layer_out = lax.psum_scatter(partial_layer, "cent", scatter_dimension=1, tiled=True)
    normed = ((layer_out + residual.astype(jnp.float32)) * gain).astype(jnp.bfloat16)
    partial_embed = jnp.dot(normed, proj_weight, preferred_element_type=jnp.float32)
    embed_full = lax.psum(partial_embed, "cent")
    scaled = (
        embed_full * lax.rsqrt(jnp.mean(embed_full * embed_full, axis=1, keepdims=True) + 1e-06)
    ).astype(jnp.bfloat16)
    block = lax.dynamic_slice_in_dim(scaled, lax.axis_index("cent") * LANES, LANES, axis=1)
    return cluster(block, centroids, hidden.shape[0] * lax.axis_size("dp"))


def solution(mesh):
    in_specs = (
        P("dp", "cent"),
        P("dp", "cent"),
        P("cent", "dp"),
        P("cent"),
        P("cent", None),
        P(("dp", "cent"), None),
    )
    out_specs = (P(("dp", "cent"), None), P(("dp", "cent")))
    return jax.shard_map(body, mesh=mesh, in_specs=in_specs, out_specs=out_specs, check_vma=False)
```

time: 618 us -> 453 us (0.73)
  blocking collectives: 149 us -> 0 us
  Pallas kernels: 0 us -> 95.3 us
  waiting for transfers between devices: 401 us -> 322 us
  matrix products: 37.1 us -> 10.7 us
  other arithmetic: 15.8 us -> 2.85 us
    pallas_call x0 -> x1, Pallas kernels: none -> 95.3 us  [cluster(): pl.pallas_call(functools.partial(main_kernel, rows, 256, 1.0 / (math.sqrt...]
    all_gather x1 -> x0, waiting for transfers between devices: 78.9 us -> none  [body(): gathered = lax.all_gather(scaled, 'dp', axis=0, tiled=True)]
    pmax x1 -> x0, blocking collectives: 76.1 us -> none  [body(): row_max = lax.pmax(local_max, ('dp', 'cent'))]
    psum x1 -> x0, blocking collectives: 73.3 us -> none  [body(): lax.psum(jnp.sum(jnp.exp(scores - row_max[:, None]), axis=1), ('dp', 'cen...]
    dot_general x2 -> x0, matrix products: 26.4 us -> none  [the longest x1 13.3 us: body(): lax.dot_general(prob_low, gathered, (((0,), (0,)), ((), ())), preferred_e...]
    reduce_sum x2 -> x0, other arithmetic: 12 us -> none  [the longest x1 6.01 us: body(): jnp.sum(jnp.exp(scores - row_max[:, None]), axis=1)]
  transfers between devices with their start and end apart: 4 -> 3, of which waited for: 4 -> 3; matrix products, arithmetic and copies ran while one was open for 0% -> 0% of each run, Pallas kernels for 0% -> 0%
where the time goes in v1:
time: 453 us; the launch traced here: 450 us
  waiting for transfers between devices  322 us (71%)
  Pallas kernels  95.3 us (21%)
  between operations  13.8 us (3%)
  matrix products  10.7 us (2%)
    psum x1, waiting for transfers between devices, body(): embed_full = lax.psum(partial_embed, 'cent')  113 us
    all_gather x1, waiting for transfers between devices, body(): lax.all_gather(down_weight, 'dp', axis=1, tiled=True)  105 us
    reduce_scatter x1, waiting for transfers between devices, body(): lax.psum_scatter(partial_layer, 'cent', scatter_dimension=1, tiled=True)  104 us
    pallas_call x1, Pallas kernels, cluster(): pl.pallas_call(functools.partial(main_kernel, rows, 256, 1.0 / (math.sqrt...  95.3 us
  transfers between devices with their start and end apart: 3, of which 3 were waited for; matrix products, arithmetic and copies ran while one was open for 0% of the time, Pallas kernels for 0%

profile of v1, /device:TPU:1, one launch (start us, length us, event | category | flops | bytes accessed | tf_op | source)
XLA Modules:
  0.0 449.6 jit_solution(16701148133362951079)
XLA Ops:
  7.2 0.0 copy-start
  7.2 0.0 copy-start.1
  7.2 0.0 copy-start.2
  7.2 0.0 all-gather.2.cloned.1.call-start
  7.2 0.7 all-gather.2.cloned.1.call-update
  7.9 0.0 reduce-scatter.2.cloned.1.call-start
  8.0 105.2 %all-gather.2.cloned.1.call-done = bf16[1376,4096]{1,0:T(8,128)(2,1)} async-done(((bf16[1376,128]{1,0:T(8,128)(2,1)}), bf16[1376,4096]{1,0:T(8,128)(2,1)}) %all-gather.2.cloned.1.call-update) | async-done | bytes 11272208 | tf_op jit(solution)/shard_map/all_gather | solution.py:306
  113.2 8.5 %fusion.3 = f32[176,4096]{1,0:T(8,128)} fusion(bf16[176,1376]{1,0:T(8,128)(2,1)} %param.6, bf16[1376,4096]{1,0:T(8,128)(2,1)} %all-gather.2.cloned.1.call-done), kind=kOutput, calls=%fused_computation.7 | convolution fusion | flops 1983905792 | bytes 14640128 | tf_op jit(solution)/shard_map/dot_general | solution.py:304
  121.7 0.0 reduce-scatter.2.cloned.1.call-update
  121.7 0.0 all-reduce.2.cloned.1.call-start
  121.8 103.8 %reduce-scatter.2.cloned.1.call-done = f32[176,512]{1,0:T(8,128)} async-done(((f32[176,4096]{1,0:T(8,128)}), f32[176,512]{1,0:T(8,128)}) %reduce-scatter.2.cloned.1.call-update) | async-done | bytes 360464 | tf_op jit(solution)/shard_map/reduce_scatter | solution.py:309
  225.6 0.0 copy-done
  225.6 0.0 copy-done.1
  225.6 0.0 copy-done.2
  225.6 2.2 fusion
  227.8 0.0 all-reduce.2.cloned.1.call-update
  227.8 112.7 %all-reduce.2.cloned.1.call-done = f32[176,1024]{1,0:T(8,128)} async-done(((f32[176,1024]{1,0:T(8,128)}), f32[176,1024]{1,0:T(8,128)}) %all-reduce.2.cloned.1.call-update) | async-done | bytes 720912 | tf_op jit(solution)/shard_map/psum | solution.py:312
  340.5 1.2 multiply_reduce_fusion
  341.8 1.6 fusion.2.block_ref
  343.4 95.3 %cluster.1 = (f32[512,1024]{1,0:T(8,128)}, f32[1,512]{1,0:T(1,128)}) custom-call(bf16[176,128]{1,0:T(8,128)(2,1)} %fusion.2.block_ref, bf16[512,1024]{1,0:T(8,128)(2,1)} %cent_ref.1), custom_call_target="tpu_custom_call" | custom-call | tf_op jit(solution)/shard_map/cluster/pallas_call | solution.py:267
  438.7 3.2 copy.11
  441.8 1.2 copy.12
  (1 shorter events, 0.0 us)
Async XLA Ops:
  7.2 218.4 %copy-start = (bf16[512,1024]{1,0:T(8,128)(2,1)S(1)}, bf16[512,1024]{1,0:T(8,128)(2,1)}, u32[]{:S(2)}) copy-start(bf16[512,1024]{1,0:T(8,128)(2,1)} %param.10) | copy-start | bytes 3145732
  7.2 218.4 %copy-start.1 = (bf16[176,512]{1,0:T(8,128)(2,1)S(1)}, bf16[176,512]{1,0:T(8,128)(2,1)}, u32[]{:S(2)}) copy-start(bf16[176,512]{1,0:T(8,128)(2,1)} %param.7) | copy-start | bytes 540676
  7.2 218.4 %copy-start.2 = (f32[512]{0:T(512)S(1)}, f32[512]{0:T(512)}, u32[]{:S(2)}) copy-start(f32[512]{0:T(512)} %param.9) | copy-start | bytes 6148
  7.2 106.0 %all-gather.2.cloned.1.call-start = ((), (), s32[]{:S(2)}) async-start(), calls=%async_computation.1 | async-start | bytes 11624448 | tf_op jit(solution)/shard_map/all_gather | solution.py:306
  7.9 217.6 %reduce-scatter.2.cloned.1.call-start = ((), (), s32[]{:S(2)}) async-start(), calls=%async_computation.2 | async-start | bytes 3244032 | tf_op jit(solution)/shard_map/reduce_scatter | solution.py:309
  121.7 218.8 %all-reduce.2.cloned.1.call-start = ((), (), s32[]{:S(2)}) async-start(), calls=%async_computation.3 | async-start | bytes 1441792 | tf_op jit(solution)/shard_map/psum | solution.py:312
Sparse Core Ops, SparseCore 0:
  9.8 103.3 all-gather.1
  121.8 103.7 reduce-scatter.1
  228.8 111.6 all-reduce.1

commit v2 on v1

--- a/solution.py
+++ b/solution.py
@@ -300,20 +300,225 @@
     return weighted, counts.reshape(per)
 
 
+def encode_kernel(
+    hidden_ref, residual_ref, down_ref, gain_ref, proj_ref, block_ref,
+    down, hid, res, layer, heard_l, sums_l, heard_f, mix, heard_m, sums_x, heard_x, sums_h, heard_h, square, squares,
+    send_sem, recv_sem, local_sem, unit_send, unit_recv,
+):
+    x, y, z, core = coordinates()
+    low, high = z % NL, z // NL
+    mate = device(x, y, z, 1 - core)
+    far = device(x, y, (z + NL) % NZ, core)
+
+    def at_x(i):
+        return device((x + i) % NX, y, z, core)
+
+    def at_far(i):
+        return device((x + i) % NX, y, (z + NL) % NZ, core)
+
+    def at_y(i):
+        return device(x, (y + i) % NY, z, core)
+
+    def at_low(i):
+        return device(x, y, high * NL + (low + i) % NL, core)
+
+    greet([mate, far, at_y(1), at_y(3)] + [f(i) for f in (at_x, at_far, at_low) for i in (1, 2, 3)])
+
+    used, done = [0], []
+
+    def remote(src, dst, target):
+        i = used[0]
+        used[0] += 1
+        copy = pltpu.make_async_remote_copy(
+            src_ref=src, dst_ref=dst, send_sem=send_sem.at[i], recv_sem=recv_sem.at[i],
+            device_id=target, device_id_type=MESH)
+        copy.start()
+        done.append(copy)
+        return copy
+
+    kept = []
+
+    def local(src, dst):
+        copy = pltpu.make_async_copy(src, dst, local_sem.at[len(kept)])
+        copy.start()
+        kept.append(copy)
+
+    units, width = down_ref.shape
+    passages = hidden_ref.shape[0]
+    pair = 2 * LANES
+
+    def tile(yc, zc, start=0, count=units):
+        return down.at[yc, zc // 2, pl.ds(start, count), pl.ds(aligned((zc % 2) * LANES, LANES), LANES)]
+
+    along_z = {i: remote(down_ref, tile(y, low), at_low(i)) for i in (1, 3, 2)}
+    ring = {0: (remote(down_ref, tile(y, low), at_y(1)), remote(down_ref, tile(y, low), at_y(3)))}
+    local(down_ref, tile(y, low))
+
+    rows = pl.ds(aligned(core * passages, 16), passages)
+    mates = pl.ds(aligned((1 - core) * passages, 16), passages)
+    from_mate = [remote(hidden_ref, hid.at[rows, :], mate)]
+    local(hidden_ref, hid.at[rows, :])
+    for b in range(2):
+        to = pl.ds(b * LANES, LANES)
+        col = aligned(b * pair + (1 - core) * LANES, LANES)
+        from_mate.append(remote(residual_ref.at[:, pl.ds(col, LANES)], res.at[rows, to], mate))
+        col = aligned(b * pair + core * LANES, LANES)
+        local(residual_ref.at[:, pl.ds(col, LANES)], res.at[rows, to])
+
+    cut = units // 32 * 16
+
+    def relay(zi):
+        zc = (low - zi + NL) % NL
+        for copy in ring[zi]:
+            copy.wait_recv()
+        lower = tile((y + 3) % NY, zc, 0, cut)
+        upper = tile((y + 1) % NY, zc, cut, units - cut)
+        return remote(lower, lower, at_y(1)), remote(upper, upper, at_y(3))
+
+    order = (0, 1, 3, 2)
+    relays = []
+    for n, zi in enumerate(order):
+        if n:
+            zc = (low - zi + NL) % NL
+            along_z[zi].wait_recv()
+            ring[zi] = (remote(tile(y, zc), tile(y, zc), at_y(1)), remote(tile(y, zc), tile(y, zc), at_y(3)))
+            relays += relay(order[n - 1])
+    for copy in kept:
+        copy.wait()
+    for copy in from_mate:
+        copy.wait_recv()
+
+    sent_units = []
+
+    def unit(o):
+        yc = (y + o) % NY
+        for h in range(2):
+            layer[yc, h] = jnp.dot(hid[...], down[yc, h], preferred_element_type=jnp.float32)
+        step = (yc - x + NX) % NX
+        slot = (step + NX - 1) % NX
+        copy = pltpu.make_async_remote_copy(
+            src_ref=layer.at[yc], dst_ref=heard_l.at[slot], send_sem=unit_send.at[o],
+            recv_sem=unit_recv.at[slot], device_id=device(yc, y, z, core), device_id_type=MESH)
+
+        @pl.when(step != 0)
+        def _():
+            copy.start()
+
+        sent_units.append((step, copy))
+
+    unit(0)
+    relays += relay(order[-1])
+    unit(1)
+    unit(3)
+    for copy in relays:
+        copy.wait_recv()
+    unit(2)
+
+    for i in range(NX - 1):
+        pltpu.make_async_remote_copy(
+            src_ref=heard_l.at[i], dst_ref=heard_l.at[i], send_sem=unit_send.at[i],
+            recv_sem=unit_recv.at[i], device_id=at_x(1), device_id_type=MESH).wait_recv()
+
+    def over_x(h):
+        value = layer[x, h]
+        for i in range(NX - 1):
+            value = value + heard_l[i, h]
+        return value
+
+    sums_l[...] = over_x(1 - high)
+    other = remote(sums_l, heard_f, far)
+    value = over_x(high)
+    other.wait_recv()
+    value = value + heard_f[...] + res[...].astype(jnp.float32)
+    gain = jnp.concatenate([gain_ref[core], gain_ref[2 + core]], axis=1)
+    normed = (value * gain).astype(jnp.bfloat16)
+    proj = jnp.concatenate(
+        [proj_ref[pl.ds(aligned(b * pair + core * LANES, LANES), LANES), :] for b in range(2)], axis=0)
+    mix[...] = jnp.dot(normed, proj, preferred_element_type=jnp.float32)
+    other = remote(mix.at[mates, :], heard_m, mate)
+    other.wait_recv()
+    wide = sums_x.shape[2]
+    for q in range(NX):
+        cols = pl.ds(q * wide, wide)
+        sums_x[q] = mix[rows, cols] + heard_m[:, cols]
+    stage = [remote(sums_x.at[(x + i) % NX], heard_x.at[i - 1], at_x(i)) for i in (1, 2, 3)]
+    for copy in stage:
+        copy.wait_recv()
+    value = sums_x[x]
+    for i in range(NX - 1):
+        value = value + heard_x[i]
+    for h in range(2):
+        sums_h[h] = value[:, h * LANES:(h + 1) * LANES]
+    remote(sums_h.at[1 - high], heard_h, far).wait_recv()
+    value = sums_h[high] + heard_h[...]
+
+    pad = square.shape[1] - passages
+    squared = jnp.concatenate([value * value, jnp.zeros((pad, LANES), jnp.float32)], axis=0)
+    square[...] = jnp.sum(squared.T, axis=0, keepdims=True)
+    stage = [remote(square, squares.at[i - 1], at_x(i)) for i in (1, 2, 3)]
+    stage += [remote(square, squares.at[3 + i], at_far(i)) for i in range(4)]
+    for copy in stage:
+        copy.wait_recv()
+    total = square[...]
+    for i in range(7):
+        total = total + squares[i]
+    norm = lax.rsqrt(total * (1.0 / proj_ref.shape[1]) + 1e-06)
+    norm = jnp.broadcast_to(norm, (LANES, norm.shape[1])).T
+    block_ref[...] = (value * norm[:passages]).astype(jnp.bfloat16)
+
+    for step, copy in sent_units:
+        @pl.when(step != 0)
+        def _():
+            copy.wait_send()
+
+    for copy in done:
+        copy.wait_send()
+
+
+def encode(hidden, residual, down_weight, gain, proj_weight):
+    passages, units = hidden.shape
+    features, embed_width = proj_weight.shape
+    vmem = pl.BlockSpec(memory_space=pltpu.VMEM)
+    hbm = pl.BlockSpec(memory_space=pl.ANY)
+    bf16, f32 = jnp.bfloat16, jnp.float32
+    pair, both = 2 * LANES, 2 * passages
+    padded = (passages + LANES - 1) // LANES * LANES
+    slots = 3 + 8 + 8 + 3 + 1 + 1 + 3 + 1 + 7
+    return pl.pallas_call(
+        encode_kernel,
+        out_shape=jax.ShapeDtypeStruct((passages, LANES), bf16),
+        in_specs=[hbm, hbm, hbm, vmem, vmem],
+        out_specs=vmem,
+        scratch_shapes=[
+            pltpu.VMEM((NY, 2, units, pair), bf16),
+            pltpu.VMEM((both, units), bf16),
+            pltpu.VMEM((both, pair), bf16),
+            pltpu.VMEM((NX, 2, both, pair), f32),
+            pltpu.VMEM((NX, 2, both, pair), f32),
+            pltpu.VMEM((both, pair), f32),
+            pltpu.VMEM((both, pair), f32),
+            pltpu.VMEM((both, embed_width), f32),
+            pltpu.VMEM((passages, embed_width), f32),
+            pltpu.VMEM((NX, passages, pair), f32),
+            pltpu.VMEM((NX - 1, passages, pair), f32),
+            pltpu.VMEM((2, passages, LANES), f32),
+            pltpu.VMEM((passages, LANES), f32),
+            pltpu.VMEM((1, padded), f32),
+            pltpu.VMEM((7, 1, padded), f32),
+            pltpu.SemaphoreType.DMA((slots,)),
+            pltpu.SemaphoreType.DMA((slots,)),
+            pltpu.SemaphoreType.DMA((4,)),
+            pltpu.SemaphoreType.DMA((NY,)),
+            pltpu.SemaphoreType.DMA((NX,)),
+        ],
+        compiler_params=pltpu.CompilerParams(
+            collective_id=1, has_side_effects=True, vmem_limit_bytes=48 * 1024 * 1024),
+        name="encode",
+    )(hidden, residual, down_weight, gain.reshape(features // LANES, 1, LANES), proj_weight)
+
+
 def body(hidden, residual, down_weight, gain, proj_weight, centroids):
-    partial_layer = jnp.dot(
-        hidden,
-        lax.all_gather(down_weight, "dp", axis=1, tiled=True),
-        preferred_element_type=jnp.float32,
-    )
-    layer_out = lax.psum_scatter(partial_layer, "cent", scatter_dimension=1, tiled=True)
-    normed = ((layer_out + residual.astype(jnp.float32)) * gain).astype(jnp.bfloat16)
-    partial_embed = jnp.dot(normed, proj_weight, preferred_element_type=jnp.float32)
-    embed_full = lax.psum(partial_embed, "cent")
-    scaled = (
-        embed_full * lax.rsqrt(jnp.mean(embed_full * embed_full, axis=1, keepdims=True) + 1e-06)
-    ).astype(jnp.bfloat16)
-    block = lax.dynamic_slice_in_dim(scaled, lax.axis_index("cent") * LANES, LANES, axis=1)
+    block = encode(hidden, residual, down_weight, gain, proj_weight)
     return cluster(block, centroids, hidden.shape[0] * lax.axis_size("dp"))
 
 

time: 453 us -> 236 us (0.52)
  waiting for transfers between devices: 322 us -> 0 us
  Pallas kernels: 95.3 us -> 223 us
  between operations: 13.8 us -> 0.68 us
  matrix products: 10.7 us -> 0 us
  local copies, waits for them, and re-layouts: 4.41 us -> 9.19 us
    pallas_call x0 -> x1, Pallas kernels: none -> 123 us  [encode(): pl.pallas_call(encode_kernel, out_shape=jax.ShapeDtypeStruct((passages, L...]
    psum x1 -> x0, waiting for transfers between devices: 113 us -> none  [body(): embed_full = lax.psum(partial_embed, 'cent')]
    all_gather x1 -> x0, waiting for transfers between devices: 105 us -> none  [body(): lax.all_gather(down_weight, 'dp', axis=1, tiled=True)]
    reduce_scatter x1 -> x0, waiting for transfers between devices: 104 us -> none  [body(): lax.psum_scatter(partial_layer, 'cent', scatter_dimension=1, tiled=True)]
    dot_general x2 -> x0, matrix products: 10.7 us -> none  [the longest x1 8.47 us: body(): jnp.dot(hidden, lax.all_gather(down_weight, 'dp', axis=1, tiled=True), pr...]
    unnamed x8 -> x16, local copies, waits for them, and re-layouts: 4.41 us -> 9.19 us
  transfers between devices with their start and end apart: 3 -> 0, of which waited for: 3 -> 0; matrix products, arithmetic and copies ran while one was open for 0% -> 0% of each run, Pallas kernels for 0% -> 0%
where the time goes in v2:
time: 236 us; the launch traced here: 233 us
  Pallas kernels  223 us (94%)
  local copies, waits for them, and re-layouts  9.19 us (4%)
    pallas_call x1, Pallas kernels, encode(): pl.pallas_call(encode_kernel, out_shape=jax.ShapeDtypeStruct((passages, L...  123 us
    pallas_call x1, Pallas kernels, cluster(): pl.pallas_call(functools.partial(main_kernel, rows, 256, 1.0 / (math.sqrt...  99.6 us
    unnamed x16, local copies, waits for them, and re-layouts  9.19 us

profile of v2, /device:TPU:1, one launch (start us, length us, event | category | flops | bytes accessed | tf_op | source)
XLA Modules:
  0.0 232.8 jit_solution(15977124603610071088)
XLA Ops:
  0.6 0.0 copy-start
  0.6 1.2 copy-done
  1.9 0.0 copy-start.1
  1.9 1.0 copy-done.1
  2.9 0.0 copy-start.2
  2.9 1.0 copy-done.2
  3.9 0.0 copy-start.3
  3.9 0.9 copy-done.3
  4.8 0.0 copy-start.5
  4.8 0.7 copy-done.5
  5.5 123.3 %encode.1.block_ref = bf16[176,128]{1,0:T(8,128)(2,1)S(1)} custom-call(bf16[176,1376]{1,0:T(8,128)(2,1)S(1)} %copy-done.1, bf16[176,512]{1,0:T(8,128)(2,1)S(1)} %copy-done.3, bf16[1376,128]{1,0:T(8,128)(2,1)S(1)} %copy-done.2, f32[4,1,128]{2,1,0:T(1,128)S(1)} %bitcast.2, bf16[512,1024]{1,0:T(8,128)(2,1)S(1)} %copy-done), custom_call_target="tpu_custom_call" | custom-call | tf_op jit(solution)/shard_map/encode/pallas_call | solution.py:487
  128.8 0.0 copy-start.4
  128.8 0.6 copy-done.4
  129.4 99.6 %cluster.1 = (f32[512,1024]{1,0:T(8,128)}, f32[1,512]{1,0:T(1,128)}) custom-call(bf16[176,128]{1,0:T(8,128)(2,1)} %copy-done.4, bf16[512,1024]{1,0:T(8,128)(2,1)} %cent_ref.1), custom_call_target="tpu_custom_call" | custom-call | tf_op jit(solution)/shard_map/cluster/pallas_call | solution.py:267
  229.1 0.0 copy-start.6
  229.1 3.2 %copy.10 = f32[512,1024]{1,0:T(8,128)} copy(f32[512,1024]{1,0:T(8,128)} %get-tuple-element.8) | data formatting | bytes 4194304
  232.3 0.0 copy-done.6
  232.3 0.6 copy.11
Async XLA Ops:
  0.6 1.2 copy-start
  1.9 1.0 copy-start.1
  2.9 1.0 copy-start.2
  3.9 0.9 copy-start.3
  4.8 0.7 copy-start.5
  128.8 0.6 copy-start.4
  229.1 3.2 %copy-start.6 = (f32[1,512]{1,0:T(1,128)S(1)}, f32[1,512]{1,0:T(1,128)}, u32[]{:S(2)}) copy-start(f32[1,512]{1,0:T(1,128)} %get-tuple-element.5) | copy-start | bytes 6148

commit v3 on v1

--- a/solution.py
+++ b/solution.py
@@ -47,19 +47,19 @@
         return ((zc // NL) * NX + xc) * LANES
 
     first = (
-        ("x", lambda i: [box(b0 + (low * NY + y) * r0, r0, (high * NX + i) * LANES, LANES)]),
-        ("y", lambda i: [box(b0 + (low * NY + i) * r0, r0, high * NX * LANES, NX * LANES)]),
-        ("z", lambda i: [box(b0 + (i % NL) * NY * r0, NY * r0, (i // NL) * NX * LANES, NX * LANES)]),
+        ("x", 2, lambda i: [box(b0 + (low * NY + y) * r0, r0, (high * NX + i) * LANES, LANES)]),
+        ("y", 2, lambda i: [box(b0 + (low * NY + i) * r0, r0, high * NX * LANES, NX * LANES)]),
+        ("z", 4, lambda i: [box(b0 + (i % NL) * NY * r0, NY * r0, (i // NL) * NX * LANES, NX * LANES)]),
     )
     second = (
-        ("y", lambda i: [box(b1 + (low * NY + i) * r1, r1, column(z, x), LANES)]),
-        ("z", lambda i: [box(b1 + (i % NL) * NY * r1, NY * r1, column(i, x), LANES)]),
-        ("x", lambda i: [box(b1, 16 * r1, (h * NX + i) * LANES, LANES) for h in range(2)]),
+        ("y", 2, lambda i: [box(b1 + (low * NY + i) * r1, r1, column(z, x), LANES)]),
+        ("z", 2, lambda i: [box(b1 + (i % NL) * NY * r1, NY * r1, column(i, x), LANES)]),
+        ("x", 2, lambda i: [box(b1, 16 * r1, (h * NX + i) * LANES, LANES) for h in range(2)]),
     )
     third = (
-        ("z", lambda i: [box(b2 + (y * NL + i % NL) * r2, r2, column(i, x), LANES)]),
-        ("x", lambda i: [box(b2 + y * NL * r2, NL * r2, (h * NX + i) * LANES, LANES) for h in range(2)]),
-        ("y", lambda i: [box(b2 + i * NL * r2, NL * r2, 0, 2 * NX * LANES)]),
+        ("z", 2, lambda i: [box(b2 + (y * NL + i % NL) * r2, r2, column(i, x), LANES)]),
+        ("x", 1, lambda i: [box(b2 + y * NL * r2, NL * r2, (h * NX + i) * LANES, LANES) for h in range(2)]),
+        ("y", 4, lambda i: [box(b2 + i * NL * r2, NL * r2, 0, 2 * NX * LANES)]),
     )
     own = (
         (0, r0, aligned(b0 + (low * NY + y) * r0, 16)),
@@ -69,26 +69,57 @@
     return (first, second, third), own, aligned(column(z, x), LANES)
 
 
-def half(box, which):
-    row, count, col, width = box
-    upper = (count // 2 + 15) // 16 * 16
-    return (row, upper, col, width) if which == 0 else (aligned(row + upper, 16), count - upper, col, width)
-
-
-def ring_steps(stages, position, size):
-    steps = []
-    for axis, boxes in stages:
-        n, me = size[axis], position[axis]
-        for s in range(1, n // 2 + 1):
-            sends = []
-            for which, way in ((0, 1), (1, -1)):
-                sent = boxes((me - way * (s - 1) + n) % n)
-                got = boxes((me - way * s + n) % n)
-                if s == n // 2:
-                    sent, got = [half(b, which) for b in sent], [half(b, which) for b in got]
-                sends.append((way, axis, sent, got))
-            steps.append(sends)
-    return steps
+def pieces(boxes, cuts):
+    out = []
+    for row, count, col, width in boxes:
+        start = 0
+        for left in range(cuts, 0, -1):
+            size = ((count - start) // 16 + left - 1) // left * 16
+            out.append((aligned(row + start, 16), size, col, width))
+            start += size
+    return out
+
+
+def ring_sends(plans, position, size):
+    sends, free = [], {}
+    hop, rate = 1.7, 45.0e3
+    for colour, stages in enumerate(plans):
+        before = []
+        for axis, cuts, boxes in stages:
+            n, me = size[axis], position[axis]
+            now, chain = [], {}
+            for s in range(1, n // 2 + 1):
+                for way in (1, -1):
+                    out = pieces(boxes((me - way * (s - 1) + n) % n), cuts)
+                    got = pieces(boxes((me - way * s + n) % n), cuts)
+                    middle = len(out) // 2
+                    keep = range(len(out))
+                    if s == n // 2:
+                        keep = keep[:middle] if way == 1 else keep[middle:]
+                    for p in keep:
+                        needs = before if s == 1 else [chain[way, s - 1, p]]
+                        chain[way, s, p] = len(sends)
+                        now.append(len(sends))
+                        sends.append((colour, axis, way, out[p], got[p], needs))
+            before = now
+    order, left, arrive = [], set(range(len(sends))), {}
+    while left:
+        best = None
+        for i in left:
+            needs = sends[i][5]
+            if all(n in arrive for n in needs):
+                start = max([arrive[n] for n in needs] + [0.0])
+                key = (max(start, free.get(sends[i][1:3], 0.0)), start, i)
+                if best is None or key < best:
+                    best = key
+        at, start, i = best
+        left.remove(i)
+        _, count, _, width = sends[i][3]
+        free[sends[i][1:3]] = at + count * width * 2 / rate
+        arrive[i] = at + count * width * 2 / rate + hop
+        order.append((start, i))
+    order.sort()
+    return sends, [i for _, i in order]
 
 
 def main_kernel(
@@ -137,34 +168,32 @@
         row, count, col, width = box
         return embed.at[pl.ds(row, count), pl.ds(col, width)]
 
-    plans = [ring_steps(stages, here, size) for stages in colours]
-    slot = 0
-    arriving, sent = [[] for _ in plans], []
-    for t in range(len(plans[0])):
-        for c, plan in enumerate(plans):
-            for copy in arriving[c]:
-                copy.wait_recv()
-            arriving[c] = []
-            for way, axis, out_boxes, in_boxes in plan[t]:
-                target = at(axis, (here[axis] + way + size[axis]) % size[axis])
-                for o, i in zip(out_boxes, in_boxes):
-                    send = pltpu.make_async_remote_copy(
-                        src_ref=view(o), dst_ref=view(o), send_sem=send_sem.at[slot],
-                        recv_sem=recv_sem.at[slot], device_id=target, device_id_type=MESH)
-                    send.start()
-                    sent.append(send)
-                    arriving[c].append(pltpu.make_async_remote_copy(
-                        src_ref=view(i), dst_ref=view(i), send_sem=send_sem.at[slot],
-                        recv_sem=recv_sem.at[slot], device_id=target, device_id_type=MESH))
-                    slot += 1
-        if t == 0:
-            share = pltpu.make_async_remote_copy(
-                src_ref=cents.at[pl.ds(mine, per), :], dst_ref=cents.at[pl.ds(mine, per), :],
-                send_sem=cent_sem.at[0], recv_sem=cent_sem.at[1], device_id=mate, device_id_type=MESH)
-            share.start()
-    for copies in arriving:
-        for copy in copies:
-            copy.wait_recv()
+    share = pltpu.make_async_remote_copy(
+        src_ref=cents.at[pl.ds(mine, per), :], dst_ref=cents.at[pl.ds(mine, per), :],
+        send_sem=cent_sem.at[0], recv_sem=cent_sem.at[1], device_id=mate, device_id_type=MESH)
+    share.start()
+    sends, order = ring_sends(colours, here, size)
+    arrived, sent = set(), []
+
+    def remote(i, piece):
+        _, axis, way = sends[i][:3]
+        return pltpu.make_async_remote_copy(
+            src_ref=view(piece), dst_ref=view(piece), send_sem=send_sem.at[i], recv_sem=recv_sem.at[i],
+            device_id=at(axis, (here[axis] + way + size[axis]) % size[axis]), device_id_type=MESH)
+
+    def hear(i):
+        if i not in arrived:
+            arrived.add(i)
+            remote(i, sends[i][4]).wait_recv()
+
+    for i in order:
+        for need in sends[i][5]:
+            hear(need)
+        copy = remote(i, sends[i][3])
+        copy.start()
+        sent.append(copy)
+    for i in order:
+        hear(i)
     for copy in sent:
         copy.wait_send()
     share.wait_send()
@@ -257,13 +286,13 @@
     per, embed_width = centroids.shape
     centres = per * lax.axis_size("dp") * lax.axis_size("cent")
     part = block.shape[0]
-    r2 = part // 3 // 16 * 16
-    r0 = (part - r2) // 2
-    rows = (r0, part - r2 - r0, r2)
+    r0 = part // 3 // 16 * 16
+    r1 = (part - r0) // 32 * 16
+    rows = (r0, r1, part - r0 - r1)
     count = passages // 2
     vmem = pl.BlockSpec(memory_space=pltpu.VMEM)
     hbm = pl.BlockSpec(memory_space=pl.ANY)
-    slots = 16 + 20 + 20
+    slots = 128
     weighted, counts = pl.pallas_call(
         functools.partial(main_kernel, rows, 256, 1.0 / (math.sqrt(embed_width) * 0.05), centres / passages),
         out_shape=(
@@ -300,20 +329,222 @@
     return weighted, counts.reshape(per)
 
 
+def encode_kernel(
+    hidden_ref, residual_ref, down_ref, gain_ref, proj_ref, block_ref,
+    down, hid, res, scale, proj, part, heard, given, heard_f, normed, turned,
+    sums_x, heard_x, sums_h, heard_h, square, squares,
+    send_sem, recv_sem, local_sem, part_send, part_recv,
+):
+    x, y, z, core = coordinates()
+    low, high = z % NL, z // NL
+    mate = device(x, y, z, 1 - core)
+    far = device(x, y, (z + NL) % NZ, core)
+    turn = device(y, x, z, core)
+    alone = x == y
+
+    def at_x(i):
+        return device((x + i) % NX, y, z, core)
+
+    def at_far(i):
+        return device((x + i) % NX, y, (z + NL) % NZ, core)
+
+    def at_y(i):
+        return device(x, (y + i) % NY, z, core)
+
+    def at_low(i):
+        return device(x, y, high * NL + (low + i) % NL, core)
+
+    peers = [mate, far] + [f(i) for f in (at_x, at_far, at_y, at_low) for i in (1, 2, 3)]
+    barrier = pltpu.get_barrier_semaphore()
+    for peer in peers:
+        pl.semaphore_signal(barrier, inc=1, device_id=peer, device_id_type=MESH)
+
+    @pl.when(jnp.logical_not(alone))
+    def _():
+        pl.semaphore_signal(barrier, inc=1, device_id=turn, device_id_type=MESH)
+
+    pl.semaphore_wait(barrier, jnp.where(alone, len(peers), len(peers) + 1))
+
+    used, done, kept = [0], [], []
+
+    def remote(src, dst, target, start=True):
+        i = used[0]
+        used[0] += 1
+        copy = pltpu.make_async_remote_copy(
+            src_ref=src, dst_ref=dst, send_sem=send_sem.at[i], recv_sem=recv_sem.at[i],
+            device_id=target, device_id_type=MESH)
+        if start:
+            copy.start()
+            done.append(copy)
+        return copy
+
+    def local(src, dst, start=True):
+        copy = pltpu.make_async_copy(src, dst, local_sem.at[len(kept)])
+        kept.append(copy)
+        if start:
+            copy.start()
+        return copy
+
+    def transposed(src, dst):
+        out, here = remote(src, dst, turn, False), local(src, dst, False)
+
+        @pl.when(jnp.logical_not(alone))
+        def _():
+            out.start()
+
+        @pl.when(alone)
+        def _():
+            here.start()
+
+        return out, here
+
+    def land(pair):
+        @pl.when(jnp.logical_not(alone))
+        def _():
+            pair[0].wait()
+
+        @pl.when(alone)
+        def _():
+            pair[1].wait()
+
+    mine = pl.ds(aligned(core * LANES, LANES), LANES)
+    passages = hidden_ref.shape[0]
+    wide = 2 * LANES
+
+    own = down.at[low, :, mine]
+    along_z = {i: remote(down_ref, own, at_low(i)) for i in (1, 3, 2)}
+    along_y = [remote(hidden_ref, hid.at[y], at_y(i)) for i in (1, 3, 2)]
+    crossed = {0: remote(down_ref, own, mate)}
+    first = [local(down_ref, own), local(hidden_ref, hid.at[y])]
+    loaded = local(proj_ref, proj)
+    moved = [transposed(residual_ref, res), transposed(gain_ref, scale)]
+
+    for copy in along_y:
+        copy.wait_recv()
+    for copy in first:
+        copy.wait()
+    flat = (NY * passages, hid.shape[2])
+    sent = []
+    for zi in (0, 1, 3, 2):
+        zc = (low - zi + NL) % NL
+        if zi:
+            along_z[zi].wait_recv()
+            crossed[zi] = remote(down.at[zc, :, mine], down.at[zc, :, mine], mate)
+        crossed[zi].wait_recv()
+        value = jnp.dot(hid[...].reshape(flat), down[zc], preferred_element_type=jnp.float32)
+        for q in range(NX):
+            part[zc, q] = value[q * passages:(q + 1) * passages]
+        for i in (1, 3, 2):
+            copy = pltpu.make_async_remote_copy(
+                src_ref=part.at[zc, (x + i) % NX], dst_ref=heard.at[zc, i - 1],
+                send_sem=part_send.at[zc, i - 1], recv_sem=part_recv.at[zc, i - 1],
+                device_id=at_x(i), device_id_type=MESH)
+            copy.start()
+            sent.append(copy)
+
+    def over_x(zc):
+        value = part[zc, x]
+        for i in (1, 3, 2):
+            pltpu.make_async_remote_copy(
+                src_ref=heard.at[zc, i - 1], dst_ref=heard.at[zc, i - 1],
+                send_sem=part_send.at[zc, i - 1], recv_sem=part_recv.at[zc, i - 1],
+                device_id=at_x(i), device_id_type=MESH).wait_recv()
+            value = value + heard[zc, i - 1]
+        return value
+
+    others = []
+    for b in range(2):
+        given[b] = over_x((1 - high) * 2 + b)
+        others.append(remote(given.at[b], heard_f.at[b], far))
+    for pair in moved:
+        land(pair)
+    for b in range(2):
+        value = over_x(high * 2 + b)
+        others[b].wait_recv()
+        cols = pl.ds(b * wide, wide)
+        gain = jnp.concatenate([scale[2 * b], scale[2 * b + 1]], axis=1)
+        value = value + heard_f[b] + res[:, cols].astype(jnp.float32)
+        normed[:, cols] = (value * gain).astype(jnp.bfloat16)
+    land(transposed(normed, turned))
+    loaded.wait()
+    mixed = jnp.dot(turned[...], proj[...], preferred_element_type=jnp.float32)
+    for q in range(NX):
+        sums_x[q] = mixed[:, q * wide:(q + 1) * wide]
+    stage = [remote(sums_x.at[(x + i) % NX], heard_x.at[i - 1], at_x(i)) for i in (1, 2, 3)]
+    for copy in stage:
+        copy.wait_recv()
+    value = sums_x[x]
+    for i in range(NX - 1):
+        value = value + heard_x[i]
+    for h in range(2):
+        sums_h[h] = value[:, h * LANES:(h + 1) * LANES]
+    remote(sums_h.at[1 - high], heard_h, far).wait_recv()
+    value = sums_h[high] + heard_h[...]
+
+    pad = square.shape[1] - passages
+    squared = jnp.concatenate([value * value, jnp.zeros((pad, LANES), jnp.float32)], axis=0)
+    square[...] = jnp.sum(squared.T, axis=0, keepdims=True)
+    stage = [remote(square, squares.at[i - 1], at_x(i)) for i in (1, 2, 3)]
+    stage += [remote(square, squares.at[3 + i], at_far(i)) for i in range(4)]
+    for copy in stage:
+        copy.wait_recv()
+    total = square[...]
+    for i in range(7):
+        total = total + squares[i]
+    norm = lax.rsqrt(total * (1.0 / proj_ref.shape[1]) + 1e-06)
+    norm = jnp.broadcast_to(norm, (LANES, norm.shape[1])).T
+    block_ref[...] = (value * norm[:passages]).astype(jnp.bfloat16)
+
+    for copy in sent + done:
+        copy.wait_send()
+
+
+def encode(hidden, residual, down_weight, gain, proj_weight):
+    passages, units = hidden.shape
+    features, embed_width = proj_weight.shape
+    vmem = pl.BlockSpec(memory_space=pltpu.VMEM)
+    hbm = pl.BlockSpec(memory_space=pl.ANY)
+    bf16, f32 = jnp.bfloat16, jnp.float32
+    wide = 2 * LANES
+    padded = (passages + LANES - 1) // LANES * LANES
+    slots = 3 + 3 + 4 + 3 + 2 + 3 + 1 + 7
+    return pl.pallas_call(
+        encode_kernel,
+        out_shape=jax.ShapeDtypeStruct((passages, LANES), bf16),
+        in_specs=[hbm, hbm, hbm, hbm, hbm],
+        out_specs=vmem,
+        scratch_shapes=[
+            pltpu.VMEM((NL, units, wide), bf16),
+            pltpu.VMEM((NY, passages, units), bf16),
+            pltpu.VMEM((passages, features), bf16),
+            pltpu.VMEM((features // LANES, 1, LANES), f32),
+            pltpu.VMEM((features, embed_width), bf16),
+            pltpu.VMEM((NL, NX, passages, wide), f32),
+            pltpu.VMEM((NL, NX - 1, passages, wide), f32),
+            pltpu.VMEM((2, passages, wide), f32),
+            pltpu.VMEM((2, passages, wide), f32),
+            pltpu.VMEM((passages, features), bf16),
+            pltpu.VMEM((passages, features), bf16),
+            pltpu.VMEM((NX, passages, wide), f32),
+            pltpu.VMEM((NX - 1, passages, wide), f32),
+            pltpu.VMEM((2, passages, LANES), f32),
+            pltpu.VMEM((passages, LANES), f32),
+            pltpu.VMEM((1, padded), f32),
+            pltpu.VMEM((7, 1, padded), f32),
+            pltpu.SemaphoreType.DMA((slots,)),
+            pltpu.SemaphoreType.DMA((slots,)),
+            pltpu.SemaphoreType.DMA((6,)),
+            pltpu.SemaphoreType.DMA((NL, NX - 1)),
+            pltpu.SemaphoreType.DMA((NL, NX - 1)),
+        ],
+        compiler_params=pltpu.CompilerParams(
+            collective_id=1, has_side_effects=True, vmem_limit_bytes=63 * 1024 * 1024),
+        name="encode",
+    )(hidden, residual, down_weight, gain.reshape(features // LANES, 1, LANES), proj_weight)
+
+
 def body(hidden, residual, down_weight, gain, proj_weight, centroids):
-    partial_layer = jnp.dot(
-        hidden,
-        lax.all_gather(down_weight, "dp", axis=1, tiled=True),
-        preferred_element_type=jnp.float32,
-    )
-    layer_out = lax.psum_scatter(partial_layer, "cent", scatter_dimension=1, tiled=True)
-    normed = ((layer_out + residual.astype(jnp.float32)) * gain).astype(jnp.bfloat16)
-    partial_embed = jnp.dot(normed, proj_weight, preferred_element_type=jnp.float32)
-    embed_full = lax.psum(partial_embed, "cent")
-    scaled = (
-        embed_full * lax.rsqrt(jnp.mean(embed_full * embed_full, axis=1, keepdims=True) + 1e-06)
-    ).astype(jnp.bfloat16)
-    block = lax.dynamic_slice_in_dim(scaled, lax.axis_index("cent") * LANES, LANES, axis=1)
+    block = encode(hidden, residual, down_weight, gain, proj_weight)
     return cluster(block, centroids, hidden.shape[0] * lax.axis_size("dp"))
 
 

time: 453 us -> 213 us (0.47)
  waiting for transfers between devices: 322 us -> 0 us
  Pallas kernels: 95.3 us -> 206 us
  between operations: 13.8 us -> 0.66 us
  matrix products: 10.7 us -> 0 us
    pallas_call x0 -> x1, Pallas kernels: none -> 119 us  [encode(): pl.pallas_call(encode_kernel, out_shape=jax.ShapeDtypeStruct((passages, L...]
    psum x1 -> x0, waiting for transfers between devices: 113 us -> none  [body(): embed_full = lax.psum(partial_embed, 'cent')]
    all_gather x1 -> x0, waiting for transfers between devices: 105 us -> none  [body(): lax.all_gather(down_weight, 'dp', axis=1, tiled=True)]
    reduce_scatter x1 -> x0, waiting for transfers between devices: 104 us -> none  [body(): lax.psum_scatter(partial_layer, 'cent', scatter_dimension=1, tiled=True)]
    dot_general x2 -> x0, matrix products: 10.7 us -> none  [the longest x1 8.47 us: body(): jnp.dot(hidden, lax.all_gather(down_weight, 'dp', axis=1, tiled=True), pr...]
    pallas_call x1, Pallas kernels: 95.3 us -> 86.5 us  [cluster(): pl.pallas_call(functools.partial(main_kernel, rows, 256, 1.0 / (math.sqrt...]
  transfers between devices with their start and end apart: 3 -> 0, of which waited for: 3 -> 0; matrix products, arithmetic and copies ran while one was open for 0% -> 0% of each run, Pallas kernels for 0% -> 0%
where the time goes in v3:
time: 213 us; the launch traced here: 210 us
  Pallas kernels  206 us (97%)
  local copies, waits for them, and re-layouts  3.74 us (2%)
    pallas_call x1, Pallas kernels, encode(): pl.pallas_call(encode_kernel, out_shape=jax.ShapeDtypeStruct((passages, L...  119 us
    pallas_call x1, Pallas kernels, cluster(): pl.pallas_call(functools.partial(main_kernel, rows, 256, 1.0 / (math.sqrt...  86.5 us

profile of v3, /device:TPU:1, one launch (start us, length us, event | category | flops | bytes accessed | tf_op | source)
XLA Modules:
  0.0 210.2 jit_solution(5471318967011547949)
XLA Ops:
  0.6 119.3 %encode.1.block_ref = bf16[176,128]{1,0:T(8,128)(2,1)} custom-call(bf16[176,1376]{1,0:T(8,128)(2,1)} %hidden_ref.1, bf16[176,512]{1,0:T(8,128)(2,1)} %residual_ref.1, bf16[1376,128]{1,0:T(8,128)(2,1)} %down_ref.1, f32[4,1,128]{2,1,0:T(1,128)} %bitcast.2, bf16[512,1024]{1,0:T(8,128)(2,1)} %proj_ref.1), custom_call_target="tpu_custom_call" | custom-call | tf_op jit(solution)/shard_map/encode/pallas_call | solution.py:511
  119.9 86.5 %cluster.1 = (f32[512,1024]{1,0:T(8,128)}, f32[1,512]{1,0:T(1,128)}) custom-call(bf16[176,128]{1,0:T(8,128)(2,1)} %encode.1.block_ref, bf16[512,1024]{1,0:T(8,128)(2,1)} %cent_ref.1), custom_call_target="tpu_custom_call" | custom-call | tf_op jit(solution)/shard_map/cluster/pallas_call | solution.py:296
  206.4 0.0 copy-start
  206.4 3.2 %copy.10 = f32[512,1024]{1,0:T(8,128)} copy(f32[512,1024]{1,0:T(8,128)} %get-tuple-element.8) | data formatting | bytes 4194304
  209.6 0.0 copy-done
  209.6 0.6 copy.11
Async XLA Ops:
  206.4 3.2 %copy-start = (f32[1,512]{1,0:T(1,128)S(1)}, f32[1,512]{1,0:T(1,128)}, u32[]{:S(2)}) copy-start(f32[1,512]{1,0:T(1,128)} %get-tuple-element.5) | copy-start | bytes 6148

commit v4 on v3

--- a/solution.py
+++ b/solution.py
@@ -331,8 +331,8 @@
 
 def encode_kernel(
     hidden_ref, residual_ref, down_ref, gain_ref, proj_ref, block_ref,
-    down, hid, res, scale, proj, part, heard, given, heard_f, normed, turned,
-    sums_x, heard_x, sums_h, heard_h, square, squares,
+    down, hid, res, scale, proj, part, relayed, heard, given, heard_f, normed, turned,
+    sums_x, relayed_x, heard_x, sums_h, heard_h, square, squares,
     send_sem, recv_sem, local_sem, part_send, part_recv,
 ):
     x, y, z, core = coordinates()
@@ -413,7 +413,7 @@
 
     own = down.at[low, :, mine]
     along_z = {i: remote(down_ref, own, at_low(i)) for i in (1, 3, 2)}
-    along_y = [remote(hidden_ref, hid.at[y], at_y(i)) for i in (1, 3, 2)]
+    along_y = [remote(hidden_ref, hid.at[y], at_y(i)) for i in (1, 3)]
     crossed = {0: remote(down_ref, own, mate)}
     first = [local(down_ref, own), local(hidden_ref, hid.at[y])]
     loaded = local(proj_ref, proj)
@@ -421,10 +421,60 @@
 
     for copy in along_y:
         copy.wait_recv()
+    upper = (passages // 2 + 15) // 16 * 16
+    lower = hid.at[(y + 3) % NY, pl.ds(0, upper), :]
+    along_y = [remote(lower, lower, at_y(1))]
+    lower = hid.at[(y + 1) % NY, pl.ds(upper, passages - upper), :]
+    along_y.append(remote(lower, lower, at_y(3)))
     for copy in first:
         copy.wait()
+    for copy in along_y:
+        copy.wait_recv()
     flat = (NY * passages, hid.shape[2])
     sent = []
+    cut = passages // 2
+    spans = (pl.ds(0, cut), pl.ds(cut, passages - cut))
+
+    def scatter(view, relay, got, send, recv):
+        def copies(i):
+            way = 1 if i % 2 == 0 else 3
+            if i < 2:
+                src, dst = view((x + 2) % NX).at[spans[i], :], relay(i)
+            else:
+                src, dst = view((x + way) % NX), got(i - 2)
+            return pltpu.make_async_remote_copy(
+                src_ref=src, dst_ref=dst, send_sem=send(i), recv_sem=recv(i),
+                device_id=at_x(way), device_id_type=MESH)
+
+        def start(i):
+            copy = copies(i)
+            copy.start()
+            sent.append(copy)
+
+        def first():
+            start(0)
+            start(1)
+
+        def second():
+            for i, way in ((0, 1), (1, 3)):
+                copies(i).wait_recv()
+                target = view((x + way) % NX)
+                target[spans[i], :] = target[spans[i], :] + relay(i)[...]
+                start(2 + i)
+
+        def finish():
+            copies(2).wait_recv()
+            copies(3).wait_recv()
+            return view(x)[...] + got(0)[...] + got(1)[...]
+
+        return first, second, finish
+
+    def block_scatter(zc):
+        return scatter(
+            lambda q: part.at[zc, q], lambda i: relayed.at[zc, i], lambda i: heard.at[zc, i],
+            lambda i: part_send.at[zc, i], lambda i: part_recv.at[zc, i])
+
+    waiting = None
     for zi in (0, 1, 3, 2):
         zc = (low - zi + NL) % NL
         if zi:
@@ -434,23 +484,15 @@
         value = jnp.dot(hid[...].reshape(flat), down[zc], preferred_element_type=jnp.float32)
         for q in range(NX):
             part[zc, q] = value[q * passages:(q + 1) * passages]
-        for i in (1, 3, 2):
-            copy = pltpu.make_async_remote_copy(
-                src_ref=part.at[zc, (x + i) % NX], dst_ref=heard.at[zc, i - 1],
-                send_sem=part_send.at[zc, i - 1], recv_sem=part_recv.at[zc, i - 1],
-                device_id=at_x(i), device_id_type=MESH)
-            copy.start()
-            sent.append(copy)
+        first, second, _ = block_scatter(zc)
+        first()
+        if waiting is not None:
+            waiting()
+        waiting = second
+    waiting()
 
     def over_x(zc):
-        value = part[zc, x]
-        for i in (1, 3, 2):
-            pltpu.make_async_remote_copy(
-                src_ref=heard.at[zc, i - 1], dst_ref=heard.at[zc, i - 1],
-                send_sem=part_send.at[zc, i - 1], recv_sem=part_recv.at[zc, i - 1],
-                device_id=at_x(i), device_id_type=MESH).wait_recv()
-            value = value + heard[zc, i - 1]
-        return value
+        return block_scatter(zc)[2]()
 
     others = []
     for b in range(2):
@@ -470,12 +512,12 @@
     mixed = jnp.dot(turned[...], proj[...], preferred_element_type=jnp.float32)
     for q in range(NX):
         sums_x[q] = mixed[:, q * wide:(q + 1) * wide]
-    stage = [remote(sums_x.at[(x + i) % NX], heard_x.at[i - 1], at_x(i)) for i in (1, 2, 3)]
-    for copy in stage:
-        copy.wait_recv()
-    value = sums_x[x]
-    for i in range(NX - 1):
-        value = value + heard_x[i]
+    first, second, finish = scatter(
+        lambda q: sums_x.at[q], lambda i: relayed_x.at[i], lambda i: heard_x.at[i],
+        lambda i: part_send.at[NL, i], lambda i: part_recv.at[NL, i])
+    first()
+    second()
+    value = finish()
     for h in range(2):
         sums_h[h] = value[:, h * LANES:(h + 1) * LANES]
     remote(sums_h.at[1 - high], heard_h, far).wait_recv()
@@ -507,7 +549,7 @@
     bf16, f32 = jnp.bfloat16, jnp.float32
     wide = 2 * LANES
     padded = (passages + LANES - 1) // LANES * LANES
-    slots = 3 + 3 + 4 + 3 + 2 + 3 + 1 + 7
+    slots = 3 + 4 + 4 + 3 + 2 + 1 + 7
     return pl.pallas_call(
         encode_kernel,
         out_shape=jax.ShapeDtypeStruct((passages, LANES), bf16),
@@ -520,13 +562,15 @@
             pltpu.VMEM((features // LANES, 1, LANES), f32),
             pltpu.VMEM((features, embed_width), bf16),
             pltpu.VMEM((NL, NX, passages, wide), f32),
-            pltpu.VMEM((NL, NX - 1, passages, wide), f32),
+            pltpu.VMEM((NL, 2, passages // 2, wide), f32),
+            pltpu.VMEM((NL, 2, passages, wide), f32),
             pltpu.VMEM((2, passages, wide), f32),
             pltpu.VMEM((2, passages, wide), f32),
             pltpu.VMEM((passages, features), bf16),
             pltpu.VMEM((passages, features), bf16),
             pltpu.VMEM((NX, passages, wide), f32),
-            pltpu.VMEM((NX - 1, passages, wide), f32),
+            pltpu.VMEM((2, passages // 2, wide), f32),
+            pltpu.VMEM((2, passages, wide), f32),
             pltpu.VMEM((2, passages, LANES), f32),
             pltpu.VMEM((passages, LANES), f32),
             pltpu.VMEM((1, padded), f32),
@@ -534,8 +578,8 @@
             pltpu.SemaphoreType.DMA((slots,)),
             pltpu.SemaphoreType.DMA((slots,)),
             pltpu.SemaphoreType.DMA((6,)),
-            pltpu.SemaphoreType.DMA((NL, NX - 1)),
-            pltpu.SemaphoreType.DMA((NL, NX - 1)),
+            pltpu.SemaphoreType.DMA((NL + 1, 4)),
+            pltpu.SemaphoreType.DMA((NL + 1, 4)),
         ],
         compiler_params=pltpu.CompilerParams(
             collective_id=1, has_side_effects=True, vmem_limit_bytes=63 * 1024 * 1024),

time: 213 us -> 209 us (0.981)
  Pallas kernels: 206 us -> 201 us
    pallas_call x1, Pallas kernels: 119 us -> 113 us  [encode(): pl.pallas_call(encode_kernel, out_shape=jax.ShapeDtypeStruct((passages, L...]
where the time goes in v4:
time: 209 us; the launch traced here: 206 us
  Pallas kernels  201 us (96%)
  local copies, waits for them, and re-layouts  3.74 us (2%)
    pallas_call x1, Pallas kernels, encode(): pl.pallas_call(encode_kernel, out_shape=jax.ShapeDtypeStruct((passages, L...  113 us
    pallas_call x1, Pallas kernels, cluster(): pl.pallas_call(functools.partial(main_kernel, rows, 256, 1.0 / (math.sqrt...  88.2 us

profile of v4, /device:TPU:1, one launch (start us, length us, event | category | flops | bytes accessed | tf_op | source)
XLA Modules:
  0.0 205.7 jit_solution(15149153310489704126)
XLA Ops:
  0.6 113.1 %encode.1.block_ref = bf16[176,128]{1,0:T(8,128)(2,1)} custom-call(bf16[176,1376]{1,0:T(8,128)(2,1)} %hidden_ref.1, bf16[176,512]{1,0:T(8,128)(2,1)} %residual_ref.1, bf16[1376,128]{1,0:T(8,128)(2,1)} %down_ref.1, f32[4,1,128]{2,1,0:T(1,128)} %bitcast.2, bf16[512,1024]{1,0:T(8,128)(2,1)} %proj_ref.1), custom_call_target="tpu_custom_call" | custom-call | tf_op jit(solution)/shard_map/encode/pallas_call | solution.py:553
  113.8 88.2 %cluster.1 = (f32[512,1024]{1,0:T(8,128)}, f32[1,512]{1,0:T(1,128)}) custom-call(bf16[176,128]{1,0:T(8,128)(2,1)} %encode.1.block_ref, bf16[512,1024]{1,0:T(8,128)(2,1)} %cent_ref.1), custom_call_target="tpu_custom_call" | custom-call | tf_op jit(solution)/shard_map/cluster/pallas_call | solution.py:296
  202.0 0.0 copy-start
  202.0 3.2 %copy.10 = f32[512,1024]{1,0:T(8,128)} copy(f32[512,1024]{1,0:T(8,128)} %get-tuple-element.8) | data formatting | bytes 4194304
  205.2 0.0 copy-done
  205.2 0.6 copy.11
Async XLA Ops:
  202.0 3.2 %copy-start = (f32[1,512]{1,0:T(1,128)S(1)}, f32[1,512]{1,0:T(1,128)}, u32[]{:S(2)}) copy-start(f32[1,512]{1,0:T(1,128)} %get-tuple-element.5) | copy-start | bytes 6148

commit v5 on v4

--- a/solution.py
+++ b/solution.py
@@ -26,13 +26,6 @@
 
 def aligned(value, multiple):
     return pl.multiple_of(value, multiple)
-
-
-def greet(peers):
-    barrier = pltpu.get_barrier_semaphore()
-    for peer in peers:
-        pl.semaphore_signal(barrier, inc=1, device_id=peer, device_id_type=MESH)
-    pl.semaphore_wait(barrier, len(peers))
 
 
 def gather_plan(rows, x, y, z):
@@ -122,56 +115,31 @@
     return sends, [i for _, i in order]
 
 
-def main_kernel(
-    rows, chunk, inverse, scale_up,
-    block_ref, cent_ref, weighted_ref, counts_ref,
-    embed, cents, expo, prob, maxima, logs, total, heard, other_sum, own_sum, other_count, sent_count,
-    send_sem, recv_sem, local_sem, cent_sem, lse_send, lse_recv, out_sem,
+def cluster(
+    rows, chunk, inverse, scale_up, value, weighted_ref, counts_ref,
+    embed, cents, expo, prob, maxima, logs, total, heard, other_sum, own_sum, kept_sum, tally, other_count, sent_count,
+    send_sem, recv_sem, lse_send, lse_recv, out_sem,
 ):
     x, y, z, core = coordinates()
     here = {"x": x, "y": y, "z": z}
     size = {"x": NX, "y": NY, "z": NZ}
+    mate = device(x, y, z, 1 - core)
+    per = weighted_ref.shape[0]
+    mine, theirs = aligned(core * per, 256), aligned((1 - core) * per, 256)
 
     def at(axis, value):
         place = dict(here)
         place[axis] = value
         return device(place["x"], place["y"], place["z"], core)
 
-    mate = device(x, y, z, 1 - core)
-    peers = [mate]
-    for axis in "xyz":
-        peers += [at(axis, (here[axis] + i) % size[axis]) for i in range(1, size[axis])]
-    greet(peers)
-
     colours, own, own_col = gather_plan(rows, x, y, z)
-    local = []
-    for i, (start, count, row) in enumerate(own):
-        local.append(pltpu.make_async_copy(
-            block_ref.at[pl.ds(start, count), :],
-            embed.at[pl.ds(row, count), pl.ds(own_col, LANES)],
-            local_sem.at[i],
-        ))
-    per = cent_ref.shape[0]
-    mine, theirs = aligned(core * per, 256), aligned((1 - core) * per, 256)
-    for c in range(8):
-        local.append(pltpu.make_async_copy(
-            cent_ref.at[:, pl.ds(c * LANES, LANES)],
-            cents.at[pl.ds(mine, per), pl.ds(((c % 2) * NX + c // 2) * LANES, LANES)],
-            local_sem.at[3 + c],
-        ))
-    for copy in local:
-        copy.start()
-    for copy in local:
-        copy.wait()
+    for start, count, row in own:
+        embed[pl.ds(row, count), pl.ds(own_col, LANES)] = value[start:start + count]
 
     def view(box):
         row, count, col, width = box
         return embed.at[pl.ds(row, count), pl.ds(col, width)]
 
-    share = pltpu.make_async_remote_copy(
-        src_ref=cents.at[pl.ds(mine, per), :], dst_ref=cents.at[pl.ds(mine, per), :],
-        send_sem=cent_sem.at[0], recv_sem=cent_sem.at[1], device_id=mate, device_id_type=MESH)
-    share.start()
     sends, order = ring_sends(colours, here, size)
     arrived, sent = set(), []
 
@@ -192,19 +160,15 @@
         copy = remote(i, sends[i][3])
         copy.start()
         sent.append(copy)
-    for i in order:
-        hear(i)
-    for copy in sent:
-        copy.wait_send()
-    share.wait_send()
-    pltpu.make_async_remote_copy(
-        src_ref=cents.at[pl.ds(theirs, per), :], dst_ref=cents.at[pl.ds(theirs, per), :],
-        send_sem=cent_sem.at[0], recv_sem=cent_sem.at[1], device_id=mate, device_id_type=MESH).wait_recv()
-
-    count = embed.shape[0]
-
-    def score(i, _):
-        span = pl.ds(aligned(i * chunk, chunk), chunk)
+
+    groups, start = [], 0
+    for r in rows:
+        groups.append((start, NY * NL * r))
+        start += NY * NL * r
+
+    def score(g):
+        start, count = groups[g]
+        span = pl.ds(start, count)
         scores = lax.dot_general(
             cents[...], embed[span, :], (((1,), (1,)), ((), ())), preferred_element_type=jnp.float32
         ) * inverse
@@ -213,124 +177,131 @@
         expo[:, span] = powers
         maxima[:, span] = top
         logs[:, span] = top + jnp.log(jnp.sum(powers, axis=0, keepdims=True))
-        return 0
-
-    lax.fori_loop(0, count // chunk, score, 0)
-
-    base = 0
-    for stage, axis in enumerate("xyz"):
-        n, me = size[axis], here[axis]
-        source = logs if stage == 0 else total.at[stage - 1]
+
+    bases = {"x": 0, "y": NX - 1, "z": NX + NY - 2}
+
+    def exchange(g, stage):
+        axis, span = "xyz"[stage], pl.ds(*groups[g])
+        source = (logs if stage == 0 else total.at[stage - 1]).at[:, span]
         copies = []
-        for i in range(1, n):
+        for i in range(1, size[axis]):
+            slot = bases[axis] + i - 1
             copies.append(pltpu.make_async_remote_copy(
-                src_ref=source, dst_ref=heard.at[base + i - 1], send_sem=lse_send.at[base + i - 1],
-                recv_sem=lse_recv.at[base + i - 1], device_id=at(axis, (me + i) % n), device_id_type=MESH))
-        for copy in copies:
+                src_ref=source, dst_ref=heard.at[slot, :, span], send_sem=lse_send.at[g, slot],
+                recv_sem=lse_recv.at[g, slot], device_id=at(axis, (here[axis] + i) % size[axis]),
+                device_id_type=MESH))
+        return source, copies
+
+    def tell(g, stage):
+        for copy in exchange(g, stage)[1]:
             copy.start()
+            sent.append(copy)
+
+    def learn(g, stage):
+        source, copies = exchange(g, stage)
+        span = pl.ds(*groups[g])
         for copy in copies:
             copy.wait_recv()
-        parts = [source[...]] + [heard[base + i] for i in range(n - 1)]
+        base = bases["xyz"[stage]]
+        parts = [source[...]] + [heard[base + i, :, span] for i in range(len(copies))]
         top = functools.reduce(jnp.maximum, parts)
-        total[stage] = top + jnp.log(sum(jnp.exp(p - top) for p in parts))
-        for copy in copies:
-            copy.wait_send()
-        base += n - 1
-    maxima[...] = jnp.exp(maxima[...] - total[2])
-
-    width = cents.shape[0]
+        total[stage, :, span] = top + jnp.log(sum(jnp.exp(p - top) for p in parts))
+
+    def weigh(g):
+        start, count = groups[g]
+        whole = pl.ds(start, count)
+        maxima[:, whole] = jnp.exp(maxima[:, whole] - total[2, :, whole])
+
+        def step(i, running):
+            span = pl.ds(aligned(start + i * chunk, chunk), chunk)
+            p = expo[:, span] * maxima[:, span]
+            prob[:, span] = p.astype(jnp.bfloat16)
+            return running + sum(p[:, j * LANES:(j + 1) * LANES] for j in range(chunk // LANES))
+
+        first = jnp.zeros(tally.shape, jnp.float32) if g == 0 else tally[...]
+        tally[...] = lax.fori_loop(0, count // chunk, step, first)
+
     lanes = 256
 
-    def weigh(i, tally):
-        span = pl.ds(aligned(i * chunk, chunk), chunk)
-        p = expo[:, span] * maxima[:, span]
-        prob[:, span] = p.astype(jnp.bfloat16)
-        return tally + sum(p[:, j * LANES:(j + 1) * LANES] for j in range(chunk // LANES))
-
-    tally = lax.fori_loop(0, count // chunk, weigh, jnp.zeros((width, LANES), jnp.float32))
-    tally = scale_up * jnp.sum(tally.T, axis=0, keepdims=True)
-    sent_count[...] = tally
-
-    def product(start, j):
-        return scale_up * lax.dot_general(
-            prob[pl.ds(start, per), :], embed[:, j * lanes:(j + 1) * lanes],
+    def product(g, first, j):
+        start, count = groups[g]
+        return lax.dot_general(
+            prob[pl.ds(first, per), pl.ds(start, count)], embed[pl.ds(start, count), j * lanes:(j + 1) * lanes],
             (((1,), (0,)), ((), ())), preferred_element_type=jnp.float32)
 
-    give = []
-    for j in range(embed.shape[1] // lanes):
+    blocks = embed.shape[1] // lanes
+
+    def accumulate(g):
+        for j in range(blocks):
+            cols = pl.ds(j * lanes, lanes)
+            for first, ref in ((theirs, own_sum), (mine, kept_sum)):
+                value = product(g, first, j)
+                ref[:, cols] = value if g == 0 else ref[:, cols] + value
+
+    def ends(c):
+        for i in order:
+            if sends[i][0] == c:
+                hear(i)
+
+    ends(0)
+    score(0)
+    tell(0, 0)
+    ends(1)
+    score(1)
+    tell(1, 0)
+    learn(0, 0)
+    tell(0, 1)
+    ends(2)
+    score(2)
+    tell(2, 0)
+    learn(1, 0)
+    tell(1, 1)
+    learn(0, 1)
+    tell(0, 2)
+    learn(2, 0)
+    tell(2, 1)
+    learn(1, 1)
+    tell(1, 2)
+    learn(0, 2)
+    weigh(0)
+    learn(2, 1)
+    tell(2, 2)
+    accumulate(0)
+    learn(1, 2)
+    weigh(1)
+    accumulate(1)
+    learn(2, 2)
+    weigh(2)
+    sent_count[...] = scale_up * jnp.sum(tally[...].T, axis=0, keepdims=True)
+
+    give = [pltpu.make_async_remote_copy(
+        src_ref=sent_count, dst_ref=other_count, send_sem=out_sem.at[0, blocks],
+        recv_sem=out_sem.at[1, blocks], device_id=mate, device_id_type=MESH)]
+    give[0].start()
+    for j in range(blocks):
         cols = pl.ds(j * lanes, lanes)
-        own_sum[:, cols] = product(theirs, j)
+        own_sum[:, cols] = scale_up * (own_sum[:, cols] + product(2, theirs, j))
         give.append(pltpu.make_async_remote_copy(
             src_ref=own_sum.at[:, cols], dst_ref=other_sum.at[:, cols], send_sem=out_sem.at[0, j],
             recv_sem=out_sem.at[1, j], device_id=mate, device_id_type=MESH))
         give[-1].start()
-    give.append(pltpu.make_async_remote_copy(
-        src_ref=sent_count, dst_ref=other_count, send_sem=out_sem.at[0, 4],
-        recv_sem=out_sem.at[1, 4], device_id=mate, device_id_type=MESH))
-    give[-1].start()
-    for j in range(embed.shape[1] // lanes):
-        part = product(mine, j)
-        give[j].wait_recv()
-        part = part + other_sum[:, j * lanes:(j + 1) * lanes]
+    for j in range(blocks):
+        cols = pl.ds(j * lanes, lanes)
+        part = scale_up * (kept_sum[:, cols] + product(2, mine, j))
+        give[1 + j].wait_recv()
+        part = part + other_sum[:, cols]
         for b in range(lanes // LANES):
             q = j * (lanes // LANES) + b
             c = (q % NX) * 2 + q // NX
             weighted_ref[:, c * LANES:(c + 1) * LANES] = part[:, b * LANES:(b + 1) * LANES]
-    give[-1].wait_recv()
+    give[0].wait_recv()
     counts_ref[...] = sent_count[:, pl.ds(mine, per)] + other_count[:, pl.ds(mine, per)]
-    for copy in give:
+    for copy in give + sent:
         copy.wait_send()
 
 
-def cluster(block, centroids, passages):
-    per, embed_width = centroids.shape
-    centres = per * lax.axis_size("dp") * lax.axis_size("cent")
-    part = block.shape[0]
-    r0 = part // 3 // 16 * 16
-    r1 = (part - r0) // 32 * 16
-    rows = (r0, r1, part - r0 - r1)
-    count = passages // 2
-    vmem = pl.BlockSpec(memory_space=pltpu.VMEM)
-    hbm = pl.BlockSpec(memory_space=pl.ANY)
-    slots = 128
-    weighted, counts = pl.pallas_call(
-        functools.partial(main_kernel, rows, 256, 1.0 / (math.sqrt(embed_width) * 0.05), centres / passages),
-        out_shape=(
-            jax.ShapeDtypeStruct((per, embed_width), jnp.float32),
-            jax.ShapeDtypeStruct((1, per), jnp.float32),
-        ),
-        in_specs=[hbm, hbm],
-        out_specs=(vmem, vmem),
-        scratch_shapes=[
-            pltpu.VMEM((count, embed_width), jnp.bfloat16),
-            pltpu.VMEM((2 * per, embed_width), jnp.bfloat16),
-            pltpu.VMEM((2 * per, count), jnp.float32),
-            pltpu.VMEM((2 * per, count), jnp.bfloat16),
-            pltpu.VMEM((1, count), jnp.float32),
-            pltpu.VMEM((1, count), jnp.float32),
-            pltpu.VMEM((3, 1, count), jnp.float32),
-            pltpu.VMEM((NX + NY + NZ - 3, 1, count), jnp.float32),
-            pltpu.VMEM((per, embed_width), jnp.float32),
-            pltpu.VMEM((per, embed_width), jnp.float32),
-            pltpu.VMEM((1, 2 * per), jnp.float32),
-            pltpu.VMEM((1, 2 * per), jnp.float32),
-            pltpu.SemaphoreType.DMA((slots,)),
-            pltpu.SemaphoreType.DMA((slots,)),
-            pltpu.SemaphoreType.DMA((11,)),
-            pltpu.SemaphoreType.DMA((2,)),
-            pltpu.SemaphoreType.DMA((NX + NY + NZ - 3,)),
-            pltpu.SemaphoreType.DMA((NX + NY + NZ - 3,)),
-            pltpu.SemaphoreType.DMA((2, 5)),
-        ],
-        compiler_params=pltpu.CompilerParams(
-            collective_id=0, has_side_effects=True, vmem_limit_bytes=60 * 1024 * 1024),
-        name="cluster",
-    )(block, centroids)
-    return weighted, counts.reshape(per)
-
-
-def encode_kernel(
-    hidden_ref, residual_ref, down_ref, gain_ref, proj_ref, block_ref,
+def encode(
+    early, later, hidden_ref, residual_ref, down_ref, gain_ref, proj_ref,
     down, hid, res, scale, proj, part, relayed, heard, given, heard_f, normed, turned,
     sums_x, relayed_x, heard_x, sums_h, heard_h, square, squares,
     send_sem, recv_sem, local_sem, part_send, part_recv,
@@ -354,7 +325,8 @@
     def at_low(i):
         return device(x, y, high * NL + (low + i) % NL, core)
 
-    peers = [mate, far] + [f(i) for f in (at_x, at_far, at_y, at_low) for i in (1, 2, 3)]
+    peers = [mate] + [f(i) for f in (at_x, at_far, at_y) for i in (1, 2, 3)]
+    peers += [device(x, y, (z + i) % NZ, core) for i in range(1, NZ)]
     barrier = pltpu.get_barrier_semaphore()
     for peer in peers:
         pl.semaphore_signal(barrier, inc=1, device_id=peer, device_id_type=MESH)
@@ -418,6 +390,7 @@
     first = [local(down_ref, own), local(hidden_ref, hid.at[y])]
     loaded = local(proj_ref, proj)
     moved = [transposed(residual_ref, res), transposed(gain_ref, scale)]
+    early()
 
     for copy in along_y:
         copy.wait_recv()
@@ -494,6 +467,7 @@
     def over_x(zc):
         return block_scatter(zc)[2]()
 
+    later()
     others = []
     for b in range(2):
         given[b] = over_x((1 - high) * 2 + b)
@@ -535,61 +509,125 @@
         total = total + squares[i]
     norm = lax.rsqrt(total * (1.0 / proj_ref.shape[1]) + 1e-06)
     norm = jnp.broadcast_to(norm, (LANES, norm.shape[1])).T
-    block_ref[...] = (value * norm[:passages]).astype(jnp.bfloat16)
-
     for copy in sent + done:
         copy.wait_send()
-
-
-def encode(hidden, residual, down_weight, gain, proj_weight):
+    return (value * norm[:passages]).astype(jnp.bfloat16)
+
+
+def whole_kernel(
+    split, plan, hidden_ref, residual_ref, down_ref, gain_ref, proj_ref, cent_ref, weighted_ref, counts_ref, *scratch,
+):
+    cent_local, cent_sem, *scratch = scratch
+    encoder, rest = scratch[:split], scratch[split:]
+    cents = rest[1]
+    x, y, z, core = coordinates()
+    per = cent_ref.shape[0]
+    mine, theirs = (pl.ds(aligned(c * per, 256), per) for c in (core, 1 - core))
+
+    def shared(rows):
+        return pltpu.make_async_remote_copy(
+            src_ref=cents.at[rows, :], dst_ref=cents.at[rows, :], send_sem=cent_sem.at[0],
+            recv_sem=cent_sem.at[1], device_id=device(x, y, z, 1 - core), device_id_type=MESH)
+
+    copies = [
+        pltpu.make_async_copy(
+            cent_ref.at[:, pl.ds(c * LANES, LANES)],
+            cents.at[mine, pl.ds(((c % 2) * NX + c // 2) * LANES, LANES)],
+            cent_local.at[c])
+        for c in range(2 * NX)
+    ]
+
+    def early():
+        for copy in copies:
+            copy.start()
+
+    def later():
+        for copy in copies:
+            copy.wait()
+        shared(mine).start()
+
+    value = encode(early, later, hidden_ref, residual_ref, down_ref, gain_ref, proj_ref, *encoder)
+    shared(theirs).wait_recv()
+    shared(mine).wait_send()
+    cluster(*plan, value, weighted_ref, counts_ref, *rest)
+
+
+def body(hidden, residual, down_weight, gain, proj_weight, centroids):
     passages, units = hidden.shape
     features, embed_width = proj_weight.shape
+    per = centroids.shape[0]
+    everyone = passages * lax.axis_size("dp")
+    centres = per * lax.axis_size("dp") * lax.axis_size("cent")
+    r0 = passages // 3 // 16 * 16
+    r1 = (passages - r0) // 32 * 16
+    rows = (r0, r1, passages - r0 - r1)
+    count = everyone // 2
+    bf16, f32 = jnp.bfloat16, jnp.float32
     vmem = pl.BlockSpec(memory_space=pltpu.VMEM)
     hbm = pl.BlockSpec(memory_space=pl.ANY)
-    bf16, f32 = jnp.bfloat16, jnp.float32
     wide = 2 * LANES
     padded = (passages + LANES - 1) // LANES * LANES
     slots = 3 + 4 + 4 + 3 + 2 + 1 + 7
-    return pl.pallas_call(
-        encode_kernel,
-        out_shape=jax.ShapeDtypeStruct((passages, LANES), bf16),
-        in_specs=[hbm, hbm, hbm, hbm, hbm],
-        out_specs=vmem,
-        scratch_shapes=[
-            pltpu.VMEM((NL, units, wide), bf16),
-            pltpu.VMEM((NY, passages, units), bf16),
-            pltpu.VMEM((passages, features), bf16),
-            pltpu.VMEM((features // LANES, 1, LANES), f32),
-            pltpu.VMEM((features, embed_width), bf16),
-            pltpu.VMEM((NL, NX, passages, wide), f32),
-            pltpu.VMEM((NL, 2, passages // 2, wide), f32),
-            pltpu.VMEM((NL, 2, passages, wide), f32),
-            pltpu.VMEM((2, passages, wide), f32),
-            pltpu.VMEM((2, passages, wide), f32),
-            pltpu.VMEM((passages, features), bf16),
-            pltpu.VMEM((passages, features), bf16),
-            pltpu.VMEM((NX, passages, wide), f32),
-            pltpu.VMEM((2, passages // 2, wide), f32),
-            pltpu.VMEM((2, passages, wide), f32),
-            pltpu.VMEM((2, passages, LANES), f32),
-            pltpu.VMEM((passages, LANES), f32),
-            pltpu.VMEM((1, padded), f32),
-            pltpu.VMEM((7, 1, padded), f32),
-            pltpu.SemaphoreType.DMA((slots,)),
-            pltpu.SemaphoreType.DMA((slots,)),
-            pltpu.SemaphoreType.DMA((6,)),
-            pltpu.SemaphoreType.DMA((NL + 1, 4)),
-            pltpu.SemaphoreType.DMA((NL + 1, 4)),
-        ],
+    hops = NX + NY + NZ - 3
+    encoder = [
+        pltpu.VMEM((NL, units, wide), bf16),
+        pltpu.VMEM((NY, passages, units), bf16),
+        pltpu.VMEM((passages, features), bf16),
+        pltpu.VMEM((features // LANES, 1, LANES), f32),
+        pltpu.VMEM((features, embed_width), bf16),
+        pltpu.VMEM((NL, NX, passages, wide), f32),
+        pltpu.VMEM((NL, 2, passages // 2, wide), f32),
+        pltpu.VMEM((NL, 2, passages, wide), f32),
+        pltpu.VMEM((2, passages, wide), f32),
+        pltpu.VMEM((2, passages, wide), f32),
+        pltpu.VMEM((passages, features), bf16),
+        pltpu.VMEM((passages, features), bf16),
+        pltpu.VMEM((NX, passages, wide), f32),
+        pltpu.VMEM((2, passages // 2, wide), f32),
+        pltpu.VMEM((2, passages, wide), f32),
+        pltpu.VMEM((2, passages, LANES), f32),
+        pltpu.VMEM((passages, LANES), f32),
+        pltpu.VMEM((1, padded), f32),
+        pltpu.VMEM((7, 1, padded), f32),
+        pltpu.SemaphoreType.DMA((slots,)),
+        pltpu.SemaphoreType.DMA((slots,)),
+        pltpu.SemaphoreType.DMA((6,)),
+        pltpu.SemaphoreType.DMA((NL + 1, 4)),
+        pltpu.SemaphoreType.DMA((NL + 1, 4)),
+    ]
+    rest = [
+        pltpu.VMEM((count, embed_width), bf16),
+        pltpu.VMEM((2 * per, embed_width), bf16),
+        pltpu.VMEM((2 * per, count), f32),
+        pltpu.VMEM((2 * per, count), bf16),
+        pltpu.VMEM((1, count), f32),
+        pltpu.VMEM((1, count), f32),
+        pltpu.VMEM((3, 1, count), f32),
+        pltpu.VMEM((hops, 1, count), f32),
+        pltpu.VMEM((per, embed_width), f32),
+        pltpu.VMEM((per, embed_width), f32),
+        pltpu.VMEM((per, embed_width), f32),
+        pltpu.VMEM((2 * per, LANES), f32),
+        pltpu.VMEM((1, 2 * per), f32),
+        pltpu.VMEM((1, 2 * per), f32),
+        pltpu.SemaphoreType.DMA((128,)),
+        pltpu.SemaphoreType.DMA((128,)),
+        pltpu.SemaphoreType.DMA((3, hops)),
+        pltpu.SemaphoreType.DMA((3, hops)),
+        pltpu.SemaphoreType.DMA((2, 5)),
+    ]
+    plan = (rows, 256, 1.0 / (math.sqrt(embed_width) * 0.05), centres / everyone)
+    weighted, counts = pl.pallas_call(
+        functools.partial(whole_kernel, len(encoder), plan),
+        out_shape=(jax.ShapeDtypeStruct((per, embed_width), f32), jax.ShapeDtypeStruct((1, per), f32)),
+        in_specs=[hbm] * 6,
+        out_specs=(vmem, vmem),
+        scratch_shapes=[pltpu.SemaphoreType.DMA((2 * NX,)), pltpu.SemaphoreType.DMA((2,))] + encoder + rest,
         compiler_params=pltpu.CompilerParams(
-            collective_id=1, has_side_effects=True, vmem_limit_bytes=63 * 1024 * 1024),
-        name="encode",
-    )(hidden, residual, down_weight, gain.reshape(features // LANES, 1, LANES), proj_weight)
-
-
-def body(hidden, residual, down_weight, gain, proj_weight, centroids):
-    block = encode(hidden, residual, down_weight, gain, proj_weight)
-    return cluster(block, centroids, hidden.shape[0] * lax.axis_size("dp"))
+            collective_id=0, has_side_effects=True, vmem_limit_bytes=63 * 1024 * 1024),
+        name="soft_kmeans",
+    )(hidden, residual, down_weight, gain.reshape(features // LANES, 1, LANES), proj_weight, centroids)
+    return weighted, counts.reshape(per)
 
 
 def solution(mesh):

time: 209 us -> 190 us (0.909); the launches traced: 206 us -> 190 us
  Pallas kernels: 201 us -> 185 us
    pallas_call x2 -> x1, Pallas kernels: 201 us -> 185 us  [body(): pl.pallas_call(functools.partial(whole_kernel, len(encoder), plan), out_s...]
where the time goes in v5:
time: 190 us
  Pallas kernels  185 us (97%)
  local copies, waits for them, and re-layouts  3.74 us (2%)
    pallas_call x1, Pallas kernels, body(): pl.pallas_call(functools.partial(whole_kernel, len(encoder), plan), out_s...  185 us

profile of v5, /device:TPU:1, one launch (start us, length us, event | category | flops | bytes accessed | tf_op | source)
XLA Modules:
  0.0 189.7 jit_solution(188926557227771745)
XLA Ops:
  0.6 185.4 %soft_kmeans.1 = (f32[512,1024]{1,0:T(8,128)}, f32[1,512]{1,0:T(1,128)}) custom-call(bf16[176,1376]{1,0:T(8,128)(2,1)} %hidden_ref.1, bf16[176,512]{1,0:T(8,128)(2,1)} %residual_ref.1, bf16[1376,128]{1,0:T(8,128)(2,1)} %down_ref.1, f32[4,1,128]{2,1,0:T(1,128)} %bitcast.3, bf16[512,1024]{1,0:T(8,128)(2,1)} %proj_ref.1, bf16[512,1024]{1,0:T(8,128)(2,1)} %cent_ref.1), custom_call_target="tpu_custom_call" | custom-call | tf_op jit(solution)/shard_map/soft_kmeans/pallas_call | solution.py:620
  186.0 0.0 copy-start
  186.0 3.2 %copy.10 = f32[512,1024]{1,0:T(8,128)} copy(f32[512,1024]{1,0:T(8,128)} %get-tuple-element.8) | data formatting | bytes 4194304
  189.2 0.0 copy-done
  189.2 0.6 copy.11
Async XLA Ops:
  186.0 3.2 %copy-start = (f32[1,512]{1,0:T(1,128)S(1)}, f32[1,512]{1,0:T(1,128)}, u32[]{:S(2)}) copy-start(f32[1,512]{1,0:T(1,128)} %get-tuple-element.5) | copy-start | bytes 6148

commit v6 on v5

--- a/solution.py
+++ b/solution.py
@@ -302,9 +302,9 @@
 
 def encode(
     early, later, hidden_ref, residual_ref, down_ref, gain_ref, proj_ref,
-    down, hid, res, scale, proj, part, relayed, heard, given, heard_f, normed, turned,
+    down, hid, res, scale, proj, part, relayed, heard, layer, heard_f, normed, turned,
     sums_x, relayed_x, heard_x, sums_h, heard_h, square, squares,
-    send_sem, recv_sem, local_sem, part_send, part_recv,
+    send_sem, recv_sem, local_sem, part_send, part_recv, z_send, z_recv, far_send, far_recv,
 ):
     x, y, z, core = coordinates()
     low, high = z % NL, z // NL
@@ -321,9 +321,6 @@
 
     def at_y(i):
         return device(x, (y + i) % NY, z, core)
-
-    def at_low(i):
-        return device(x, y, high * NL + (low + i) % NL, core)
 
     peers = [mate] + [f(i) for f in (at_x, at_far, at_y) for i in (1, 2, 3)]
     peers += [device(x, y, (z + i) % NZ, core) for i in range(1, NZ)]
@@ -384,7 +381,16 @@
     wide = 2 * LANES
 
     own = down.at[low, :, mine]
-    along_z = {i: remote(down_ref, own, at_low(i)) for i in (1, 3, 2)}
+    near = [low, low + 1 - 2 * (low % 2), jnp.where(low < 2, 2, 1), jnp.where(low < 2, 3, 0)]
+
+    def along_z(source, target):
+        block = down.at[source, :, mine]
+        return pltpu.make_async_remote_copy(
+            src_ref=down_ref, dst_ref=block, send_sem=z_send.at[target], recv_sem=z_recv.at[source],
+            device_id=device(x, y, high * NL + target, core), device_id_type=MESH)
+
+    for target in near[1:]:
+        along_z(low, target).start()
     along_y = [remote(hidden_ref, hid.at[y], at_y(i)) for i in (1, 3)]
     crossed = {0: remote(down_ref, own, mate)}
     first = [local(down_ref, own), local(hidden_ref, hid.at[y])]
@@ -447,36 +453,41 @@
             lambda q: part.at[zc, q], lambda i: relayed.at[zc, i], lambda i: heard.at[zc, i],
             lambda i: part_send.at[zc, i], lambda i: part_recv.at[zc, i])
 
-    waiting = None
-    for zi in (0, 1, 3, 2):
-        zc = (low - zi + NL) % NL
-        if zi:
-            along_z[zi].wait_recv()
-            crossed[zi] = remote(down.at[zc, :, mine], down.at[zc, :, mine], mate)
-        crossed[zi].wait_recv()
+    def far_copy(zc):
+        return pltpu.make_async_remote_copy(
+            src_ref=layer.at[zc], dst_ref=heard_f.at[zc % 2], send_sem=far_send.at[zc % 2],
+            recv_sem=far_recv.at[zc % 2], device_id=far, device_id_type=MESH)
+
+    def third(zc):
+        layer[zc] = block_scatter(zc)[2]()
+
+        @pl.when(zc // 2 != high)
+        def _():
+            far_copy(zc).start()
+
+    for n, zc in enumerate(near):
+        if n:
+            along_z(zc, zc).wait_recv()
+            crossed[n] = remote(down.at[zc, :, mine], down.at[zc, :, mine], mate)
+        crossed[n].wait_recv()
         value = jnp.dot(hid[...].reshape(flat), down[zc], preferred_element_type=jnp.float32)
         for q in range(NX):
             part[zc, q] = value[q * passages:(q + 1) * passages]
-        first, second, _ = block_scatter(zc)
-        first()
-        if waiting is not None:
-            waiting()
-        waiting = second
-    waiting()
-
-    def over_x(zc):
-        return block_scatter(zc)[2]()
+        block_scatter(zc)[0]()
+        if n > 0:
+            block_scatter(near[n - 1])[1]()
+        if n > 1:
+            third(near[n - 2])
+    block_scatter(near[3])[1]()
+    third(near[2])
+    third(near[3])
 
     later()
-    others = []
-    for b in range(2):
-        given[b] = over_x((1 - high) * 2 + b)
-        others.append(remote(given.at[b], heard_f.at[b], far))
     for pair in moved:
         land(pair)
     for b in range(2):
-        value = over_x(high * 2 + b)
-        others[b].wait_recv()
+        value = layer[high * 2 + b]
+        far_copy(high * 2 + b).wait_recv()
         cols = pl.ds(b * wide, wide)
         gain = jnp.concatenate([scale[2 * b], scale[2 * b + 1]], axis=1)
         value = value + heard_f[b] + res[:, cols].astype(jnp.float32)
@@ -509,6 +520,10 @@
         total = total + squares[i]
     norm = lax.rsqrt(total * (1.0 / proj_ref.shape[1]) + 1e-06)
     norm = jnp.broadcast_to(norm, (LANES, norm.shape[1])).T
+    for target in near[1:]:
+        along_z(low, target).wait_send()
+    for b in range(2):
+        far_copy((1 - high) * 2 + b).wait_send()
     for copy in sent + done:
         copy.wait_send()
     return (value * norm[:passages]).astype(jnp.bfloat16)
@@ -578,7 +593,7 @@
         pltpu.VMEM((NL, NX, passages, wide), f32),
         pltpu.VMEM((NL, 2, passages // 2, wide), f32),
         pltpu.VMEM((NL, 2, passages, wide), f32),
-        pltpu.VMEM((2, passages, wide), f32),
+        pltpu.VMEM((NL, passages, wide), f32),
         pltpu.VMEM((2, passages, wide), f32),
         pltpu.VMEM((passages, features), bf16),
         pltpu.VMEM((passages, features), bf16),
@@ -594,6 +609,10 @@
         pltpu.SemaphoreType.DMA((6,)),
         pltpu.SemaphoreType.DMA((NL + 1, 4)),
         pltpu.SemaphoreType.DMA((NL + 1, 4)),
+        pltpu.SemaphoreType.DMA((NL,)),
+        pltpu.SemaphoreType.DMA((NL,)),
+        pltpu.SemaphoreType.DMA((2,)),
+        pltpu.SemaphoreType.DMA((2,)),
     ]
     rest = [
         pltpu.VMEM((count, embed_width), bf16),

time: 190 us -> 186 us (0.979)
  Pallas kernels: 185 us -> 181 us
    pallas_call x1, Pallas kernels: 185 us -> 181 us  [body(): pl.pallas_call(functools.partial(whole_kernel, len(encoder), plan), out_s...]
where the time goes in v6:
time: 186 us
  Pallas kernels  181 us (97%)
  local copies, waits for them, and re-layouts  3.74 us (2%)
    pallas_call x1, Pallas kernels, body(): pl.pallas_call(functools.partial(whole_kernel, len(encoder), plan), out_s...  181 us
    unnamed x4, local copies, waits for them, and re-layouts  3.74 us

profile of v6, /device:TPU:1, one launch (start us, length us, event | category | flops | bytes accessed | tf_op | source)
XLA Modules:
  0.0 185.9 jit_solution(15551308454889128727)
XLA Ops:
  0.6 181.5 %soft_kmeans.1 = (f32[512,1024]{1,0:T(8,128)}, f32[1,512]{1,0:T(1,128)}) custom-call(bf16[176,1376]{1,0:T(8,128)(2,1)} %hidden_ref.1, bf16[176,512]{1,0:T(8,128)(2,1)} %residual_ref.1, bf16[1376,128]{1,0:T(8,128)(2,1)} %down_ref.1, f32[4,1,128]{2,1,0:T(1,128)} %bitcast.3, bf16[512,1024]{1,0:T(8,128)(2,1)} %proj_ref.1, bf16[512,1024]{1,0:T(8,128)(2,1)} %cent_ref.1), custom_call_target="tpu_custom_call" | custom-call | tf_op jit(solution)/shard_map/soft_kmeans/pallas_call | solution.py:639
  182.1 0.0 copy-start
  182.1 3.2 %copy.10 = f32[512,1024]{1,0:T(8,128)} copy(f32[512,1024]{1,0:T(8,128)} %get-tuple-element.8) | data formatting | bytes 4194304
  185.3 0.0 copy-done
  185.3 0.6 copy.11
Async XLA Ops:
  182.1 3.2 %copy-start = (f32[1,512]{1,0:T(1,128)S(1)}, f32[1,512]{1,0:T(1,128)}, u32[]{:S(2)}) copy-start(f32[1,512]{1,0:T(1,128)} %get-tuple-element.5) | copy-start | bytes 6148

commit v7 on v6

--- a/solution.py
+++ b/solution.py
@@ -485,6 +485,7 @@
     later()
     for pair in moved:
         land(pair)
+    turning = []
     for b in range(2):
         value = layer[high * 2 + b]
         far_copy(high * 2 + b).wait_recv()
@@ -492,9 +493,13 @@
         gain = jnp.concatenate([scale[2 * b], scale[2 * b + 1]], axis=1)
         value = value + heard_f[b] + res[:, cols].astype(jnp.float32)
         normed[:, cols] = (value * gain).astype(jnp.bfloat16)
-    land(transposed(normed, turned))
+        turning.append(transposed(normed.at[:, cols], turned.at[:, cols]))
     loaded.wait()
-    mixed = jnp.dot(turned[...], proj[...], preferred_element_type=jnp.float32)
+    mixed = 0.0
+    for b in range(2):
+        cols = pl.ds(b * wide, wide)
+        land(turning[b])
+        mixed = mixed + jnp.dot(turned[:, cols], proj[cols, :], preferred_element_type=jnp.float32)
     for q in range(NX):
         sums_x[q] = mixed[:, q * wide:(q + 1) * wide]
     first, second, finish = scatter(
@@ -582,7 +587,7 @@
     hbm = pl.BlockSpec(memory_space=pl.ANY)
     wide = 2 * LANES
     padded = (passages + LANES - 1) // LANES * LANES
-    slots = 3 + 4 + 4 + 3 + 2 + 1 + 7
+    slots = 4 + 4 + 4 + 3 + 2 + 1 + 7
     hops = NX + NY + NZ - 3
     encoder = [
         pltpu.VMEM((NL, units, wide), bf16),
@@ -606,7 +611,7 @@
         pltpu.VMEM((7, 1, padded), f32),
         pltpu.SemaphoreType.DMA((slots,)),
         pltpu.SemaphoreType.DMA((slots,)),
-        pltpu.SemaphoreType.DMA((6,)),
+        pltpu.SemaphoreType.DMA((7,)),
         pltpu.SemaphoreType.DMA((NL + 1, 4)),
         pltpu.SemaphoreType.DMA((NL + 1, 4)),
         pltpu.SemaphoreType.DMA((NL,)),

time: 186 us -> 186 us (level)
  no operation moved by 1% of the time
where the time goes in v7:
time: 186 us; the launch traced here: 185 us
  Pallas kernels  181 us (97%)
  local copies, waits for them, and re-layouts  3.74 us (2%)
    pallas_call x1, Pallas kernels, body(): pl.pallas_call(functools.partial(whole_kernel, len(encoder), plan), out_s...  181 us
    unnamed x4, local copies, waits for them, and re-layouts  3.74 us

profile of v7, /device:TPU:1, one launch (start us, length us, event | category | flops | bytes accessed | tf_op | source)
XLA Modules:
  0.0 185.4 jit_solution(12753556820290566176)
XLA Ops:
  0.6 181.0 %soft_kmeans.1 = (f32[512,1024]{1,0:T(8,128)}, f32[1,512]{1,0:T(1,128)}) custom-call(bf16[176,1376]{1,0:T(8,128)(2,1)} %hidden_ref.1, bf16[176,512]{1,0:T(8,128)(2,1)} %residual_ref.1, bf16[1376,128]{1,0:T(8,128)(2,1)} %down_ref.1, f32[4,1,128]{2,1,0:T(1,128)} %bitcast.3, bf16[512,1024]{1,0:T(8,128)(2,1)} %proj_ref.1, bf16[512,1024]{1,0:T(8,128)(2,1)} %cent_ref.1), custom_call_target="tpu_custom_call" | custom-call | tf_op jit(solution)/shard_map/soft_kmeans/pallas_call | solution.py:644
  181.7 0.0 copy-start
  181.7 3.2 %copy.10 = f32[512,1024]{1,0:T(8,128)} copy(f32[512,1024]{1,0:T(8,128)} %get-tuple-element.8) | data formatting | bytes 4194304
  184.8 0.0 copy-done
  184.8 0.6 copy.11
Async XLA Ops:
  181.7 3.2 %copy-start = (f32[1,512]{1,0:T(1,128)S(1)}, f32[1,512]{1,0:T(1,128)}, u32[]{:S(2)}) copy-start(f32[1,512]{1,0:T(1,128)} %get-tuple-element.5) | copy-start | bytes 6148
